TPU v7x, 512 devices: a whole 4x4x16 slice. The times are simulated.
512 devices in a mesh: heads: 8 (over x, core), frames: 64 (over z, y).
Axes of the slice: x: 4, y: 4, z: 16, core: 2. Of those that a mesh axis runs over, the one named last changes fastest.
Arguments:
- query_proj: bfloat16 [32768, 5120], P('frames', 'heads'), may hold values from -60 to 60
- key_proj: bfloat16 [32768, 5120], P('frames', 'heads'), may hold values from -60 to 60
- value_proj: bfloat16 [32768, 5120], P('frames', 'heads'), may hold values from -96 to 96
- query_gain: float32 [5120], P('heads'), may hold values from 0.1 to 1.9
- key_gain: float32 [5120], P('heads'), may hold values from 0.1 to 1.9
- key_blocks: int32 [64, 16], P('frames'), may hold values from 0 to 15, each once within a row
Outputs:
- attended: float32 [32768, 5120], P('frames', 'heads')
Inputs may be any that keep to these rules, and one draw needn't show every extreme that they name: `key_blocks`: each row is a permutation of the key block numbers of one frame.
All inputs are finite; a program needn't handle non-finite values.
Results may differ from a plain program's by a relative error of at most 0.012.
Values may be sent and summed in bfloat16 or wider, within the bound.
No kernel may reach another device: no remote copies, remote signals or barrier semaphores. Data moves between devices by JAX's collectives and lax.ppermute only.
A program may use at most 64 MiB of HBM per device.

v0:
```python
import jax
import jax.numpy as jnp
from jax import lax
from jax.sharding import PartitionSpec as P

HD = 128
OCTAVES = 3


EPS = 1e-06


def from_behind(value, axis, steps):
    count = lax.axis_size(axis)
    initial, last = (max(0, -steps), min(count, count - steps))
    return lax.ppermute(value, axis, [(source, source + steps) for source in range(initial, last)])


def scaled_rows(inputs, squares, width_total, gain_row):
    factor = lax.rsqrt(squares / width_total + EPS)[:, None]
    return (inputs.astype(jnp.float32) * factor * gain_row).astype(jnp.bfloat16)


def climb(own_rows, levels, upward):
    held_pieces = [own_rows]
    for octave in range(levels):
        kept_rows = own_rows.shape[2] >> octave
        packed = jnp.concatenate([piece[:, :, :kept_rows] for piece in held_pieces], axis=1)
        if upward:
            arrived = from_behind(packed, "frames", -(1 << octave))
        else:
            arrived = from_behind(packed, "frames", 1 << octave)
        held_pieces.append(arrived)
    return held_pieces[1:]


def on_device(query_proj, key_proj, value_proj, query_gain, key_gain, key_blocks):
    row_count, feature_width = query_proj.shape
    head_count = feature_width // HD
    width_total = feature_width * lax.axis_size("heads")
    frame_count = lax.axis_size("frames")
    query_float = query_proj.astype(jnp.float32)
    key_float = key_proj.astype(jnp.float32)
    query_sq, key_sq = lax.psum(
        (jnp.sum(query_float * query_float, axis=1), jnp.sum(key_float * key_float, axis=1)),
        "heads",
    )
    q_hat = scaled_rows(query_proj, query_sq, width_total, query_gain)
    k_hat = scaled_rows(key_proj, key_sq, width_total, key_gain)
    block_count = key_blocks.shape[1]
    block_size = row_count // block_count
    blocked = jnp.stack([k_hat, value_proj]).reshape(2, block_count, block_size, feature_width)
    ranked = blocked[:, key_blocks[0]].reshape(2, row_count, feature_width)
    frame_index = lax.axis_index("frames")
    upper_side = climb(ranked[:, None], OCTAVES, True)
    lower_side = climb(ranked[:, None], OCTAVES, False)
    pieces = [ranked]
    validity = [jnp.ones((row_count,), dtype=bool)]
    for octave in range(OCTAVES):
        frame_span = 1 << octave
        kept_rows = row_count >> octave
        steps_away = frame_span + jnp.arange(frame_span, dtype=jnp.int32)
        pieces.append(upper_side[octave].reshape(2, frame_span * kept_rows, feature_width))
        validity.append(jnp.repeat(frame_index + steps_away < frame_count, kept_rows))
        pieces.append(lower_side[octave].reshape(2, frame_span * kept_rows, feature_width))
        validity.append(jnp.repeat(frame_index - steps_away >= 0, kept_rows))
    joined = jnp.concatenate(pieces, axis=1)
    score_bias = jnp.where(jnp.concatenate(validity), 0.0, -1e30).astype(jnp.float32)
    joined_keys = joined[0]
    joined_values = joined[1]

    def attend_head(head):
        start = head * HD
        query_head = lax.dynamic_slice_in_dim(q_hat, start, HD, 1)
        key_head = lax.dynamic_slice_in_dim(joined_keys, start, HD, 1)
        value_head = lax.dynamic_slice_in_dim(joined_values, start, HD, 1)
        scores = (
            lax.dot_general(
                query_head, key_head, (((1,), (1,)), ((), ())), preferred_element_type=jnp.float32
            )
            * HD ** (-0.5)
            + score_bias
        )
        row_max = jnp.max(scores, axis=1, keepdims=True)
        weights = jnp.exp(scores - row_max)
        totals = jnp.sum(weights, axis=1, keepdims=True)
        mixed = jnp.dot(
            weights.astype(jnp.bfloat16), value_head, preferred_element_type=jnp.float32
        )
        return mixed / totals

    result = lax.map(attend_head, jnp.arange(head_count, dtype=jnp.int32))
    return result.transpose(1, 0, 2).reshape(row_count, feature_width)


def solution(mesh):
    placed = (
        P("frames", "heads"),
        P("frames", "heads"),
        P("frames", "heads"),
        P("heads"),
        P("heads"),
        P("frames", None),
    )
    return jax.shard_map(
        on_device, mesh=mesh, in_specs=placed, out_specs=P("frames", "heads"), check_vma=False
    )
```

profile of v0, /device:TPU:390, one launch (start us, length us, event | category | flops | bytes accessed | tf_op | source)
XLA Modules:
  0.0 217.0 jit_solution(15543560789549009485)
XLA Ops:
  0.0 1.4 fusion.16
  1.4 1.3 fusion.19
  2.7 10.5 %all-reduce = (f32[512]{0:T(512)S(1)}, f32[512]{0:T(512)S(1)}) all-reduce(f32[512]{0:T(512)S(1)} %fusion.16, f32[512]{0:T(512)S(1)} %fusion.19), channel_id=1, replica_groups=mesh['heads'=8,'frames'=64] {'heads'}, use_global_device_ids=true, to_apply=%region_1.0 | all-reduce | flops 1024 | bytes 8192 | tf_op jit(solution)/shard_map/psum | solution.py:44
  13.7 0.8 gather_fusion
  14.6 6.6 %collective-permute-start = (bf16[2,1,512,640]{3,2,0,1:T(8,128)(2,1)S(1)}, bf16[2,1,512,640]{3,2,0,1:T(8,128)(2,1)S(1)}, u32[]{:S(2)}, u32[]{:S(2)}) collective-permute-start(bf16[2,1,512,640]{3,2,0,1:T(8,128)(2,1)S(1)} %bitcast.35), channel_id=1, source_target_pairs={{1,0},{2,1},{3,2},{4,3},{5,4},{6,5},{7,6},{8,7},{9,8},{10,9},{11,1... | collective-permute-start | bytes 3932168 | tf_op jit(solution)/shard_map/ppermute | solution.py:16
  21.2 1.9 collective-permute-start.1
  23.2 27.0 %collective-permute-done = bf16[2,1,512,640]{3,2,0,1:T(8,128)(2,1)S(1)} collective-permute-done((bf16[2,1,512,640]{3,2,0,1:T(8,128)(2,1)S(1)}, bf16[2,1,512,640]{3,2,0,1:T(8,128)(2,1)S(1)}, u32[]{:S(2)}, u32[]{:S(2)}) %collective-permute-start) | collective-permute-done | bytes 1310752 | tf_op jit(solution)/shard_map/ppermute | solution.py:16
  50.2 7.8 %collective-permute-done.1 = bf16[2,1,512,640]{3,2,0,1:T(8,128)(2,1)S(1)} collective-permute-done((bf16[2,1,512,640]{3,2,0,1:T(8,128)(2,1)S(1)}, bf16[2,1,512,640]{3,2,0,1:T(8,128)(2,1)S(1)}, u32[]{:S(2)}, u32[]{:S(2)}) %collective-permute-start.1) | collective-permute-done | bytes 1310752 | tf_op jit(solution)/shard_map/ppermute | solution.py:16
  58.0 1.1 copy-done.2
  59.1 1.7 pad_maximum_fusion.2
  60.8 1.9 collective-permute-start.2
  62.8 5.4 %collective-permute-start.3 = (bf16[2,2,256,640]{3,2,0,1:T(8,128)(2,1)}, bf16[2,2,256,640]{3,2,0,1:T(8,128)(2,1)}, u32[]{:S(2)}, u32[]{:S(2)}) collective-permute-start(bf16[2,2,256,640]{3,2,0,1:T(8,128)(2,1)} %get-tuple-element.63), channel_id=1, source_target_pairs={{0,2},{1,3},{2,4},{3,5},{4,6},{5,7},{6,8},{7,9},{8,10},{9,11},{10,... | collective-permute-start | bytes 3932168 | tf_op jit(solution)/shard_map/ppermute | solution.py:16
  68.5 0.2 dynamic-update-slice
  68.7 0.2 dynamic-update-slice.1
  68.9 0.2 dynamic-update-slice.2
  70.0 53.4 %collective-permute-done.2 = bf16[2,2,256,640]{3,2,0,1:T(8,128)(2,1)} collective-permute-done((bf16[2,2,256,640]{3,2,0,1:T(8,128)(2,1)}, bf16[2,2,256,640]{3,2,0,1:T(8,128)(2,1)}, u32[]{:S(2)}, u32[]{:S(2)}) %collective-permute-start.2) | collective-permute-done | bytes 1310752 | tf_op jit(solution)/shard_map/ppermute | solution.py:16
  123.3 1.1 slice.49
  124.5 1.1 slice.51
  125.7 1.8 fusion.23
  127.5 1.9 collective-permute-start.4
  129.4 3.9 %collective-permute-start.5 = (bf16[2,4,128,640]{3,2,0,1:T(8,128)(2,1)}, bf16[2,4,128,640]{3,2,0,1:T(8,128)(2,1)}, u32[]{:S(2)}, u32[]{:S(2)}) collective-permute-start(bf16[2,4,128,640]{3,2,0,1:T(8,128)(2,1)} %get-tuple-element.65), channel_id=1, source_target_pairs={{0,4},{1,5},{2,6},{3,7},{4,8},{5,9},{6,10},{7,11},{8,12},{9,13},{1... | collective-permute-start | bytes 3932168 | tf_op jit(solution)/shard_map/ppermute | solution.py:16
  133.4 1.2 constant_dynamic-update-slice_fusion.5
  134.8 1.1 copy-done.1
  135.9 1.2 bitcast_dynamic-update-slice_fusion.1
  137.1 0.6 copy-done.3
  137.7 1.2 bitcast_dynamic-update-slice_fusion
  138.8 1.4 copy.20
  140.3 1.4 copy.21
  141.7 1.2 constant_dynamic-update-slice_fusion.4
  142.9 1.2 constant_dynamic-update-slice_fusion.3
  144.1 15.5 %collective-permute-done.4 = bf16[2,4,128,640]{3,2,0,1:T(8,128)(2,1)} collective-permute-done((bf16[2,4,128,640]{3,2,0,1:T(8,128)(2,1)}, bf16[2,4,128,640]{3,2,0,1:T(8,128)(2,1)}, u32[]{:S(2)}, u32[]{:S(2)}) %collective-permute-start.4) | collective-permute-done | bytes 1310752 | tf_op jit(solution)/shard_map/ppermute | solution.py:16
  159.6 1.4 copy.22
  161.0 1.2 constant_dynamic-update-slice_fusion.2
  162.2 0.5 collective-permute-done.5
  162.7 1.4 copy.23
  164.2 1.3 constant_dynamic-update-slice_fusion.1
  165.4 8.1 %slice_bitcast_fusion = (bf16[3584,640]{1,0:T(8,128)(2,1)}, bf16[3584,640]{1,0:T(8,128)(2,1)}) fusion(bf16[2,3584,640]{2,1,0:T(8,128)(2,1)} %constant_dynamic-update-slice_fusion.1), kind=kLoop, calls=%fused_computation.15 | loop fusion | bytes 18350080 | tf_op jit(solution)/shard_map/squeeze | solution.py:70
  173.5 40.7 %while.10 = (s32[]{:T(128)}, f32[5,512,128]{1,2,0:T(8,128)}, s32[5]{0:T(128)S(1)}, bf16[512,640]{1,0:T(8,128)(2,1)S(1)}, bf16[3584,640]{1,0:T(8,128)(2,1)}, /*in...) while((s32[]{:T(128)}, f32[5,512,128]{1,2,0:T(8,128)}, ...), condition=%wide.region_7.8_spmd, body=%wide.region_4.7_spmd.sunk | while | flops 952433664 | bytes 25325228 | solution.py:92
  173.5 0.6 dynamic_slice.30
  174.7 2.5 %fusion.33 = (f32[512]{0:T(512)S(1)}, f32[512,3584]{1,0:T(8,128)S(1)}) fusion(f32[3584]{0:T(1024)S(1)} %get-tuple-element.147, bf16[3584,640]{1,0:T(8,128)(2,1)} %get-tuple-element.146, s32[]{:T(128)S(6)} %select_n.26, bf16[512,640]{1,0:T(8,128)(2,1)S(1)} %get-tuple-element.145), kind=kOutput, calls=%fused_computation.55.clone.1 | convolution fusion | flops 475266560 | bytes 8408064 | tf_op jit(solution)/shard_map/while/body/eval_jaxpr/dot_general | solution.py:78
  177.2 1.1 fusion.34
  178.3 2.4 %fusion.35 = f32[1,512,128]{2,1,0:T(8,128)S(1)} fusion(f32[512,3584]{1,0:T(8,128)S(1)} %get-tuple-element.118, f32[512]{0:T(512)S(1)} %get-tuple-element.119, bf16[3584,640]{1,0:T(8,128)(2,1)} %get-tuple-element.148, s32[]{:T(128)S(6)} %select_n.26, f32[512]{0:T(512)S(1)} %fusion.34), kind=kOutput, calls=%fused_computation.8.clone.1 | convolution fusion | flops 473497600 | bytes 8523780 | tf_op jit(solution)/shard_map/while/body/eval_jaxpr/dot_general | solution.py:87
  180.9 0.7 constant_dynamic-update-slice_fusion.8
  181.6 0.6 dynamic_slice.30
  182.9 2.5 %fusion.33 = (f32[512]{0:T(512)S(1)}, f32[512,3584]{1,0:T(8,128)S(1)}) fusion(f32[3584]{0:T(1024)S(1)} %get-tuple-element.147, bf16[3584,640]{1,0:T(8,128)(2,1)} %get-tuple-element.146, s32[]{:T(128)S(6)} %select_n.26, bf16[512,640]{1,0:T(8,128)(2,1)S(1)} %get-tuple-element.145), kind=kOutput, calls=%fused_computation.55.clone.1 | convolution fusion | flops 475266560 | bytes 8408064 | tf_op jit(solution)/shard_map/while/body/eval_jaxpr/dot_general | solution.py:78
  185.3 1.1 fusion.34
  186.5 2.4 %fusion.35 = f32[1,512,128]{2,1,0:T(8,128)S(1)} fusion(f32[512,3584]{1,0:T(8,128)S(1)} %get-tuple-element.118, f32[512]{0:T(512)S(1)} %get-tuple-element.119, bf16[3584,640]{1,0:T(8,128)(2,1)} %get-tuple-element.148, s32[]{:T(128)S(6)} %select_n.26, f32[512]{0:T(512)S(1)} %fusion.34), kind=kOutput, calls=%fused_computation.8.clone.1 | convolution fusion | flops 473497600 | bytes 8523780 | tf_op jit(solution)/shard_map/while/body/eval_jaxpr/dot_general | solution.py:87
  189.0 0.7 constant_dynamic-update-slice_fusion.8
  189.8 0.6 dynamic_slice.30
  191.0 2.5 %fusion.33 = (f32[512]{0:T(512)S(1)}, f32[512,3584]{1,0:T(8,128)S(1)}) fusion(f32[3584]{0:T(1024)S(1)} %get-tuple-element.147, bf16[3584,640]{1,0:T(8,128)(2,1)} %get-tuple-element.146, s32[]{:T(128)S(6)} %select_n.26, bf16[512,640]{1,0:T(8,128)(2,1)S(1)} %get-tuple-element.145), kind=kOutput, calls=%fused_computation.55.clone.1 | convolution fusion | flops 475266560 | bytes 8408064 | tf_op jit(solution)/shard_map/while/body/eval_jaxpr/dot_general | solution.py:78
  193.5 1.1 fusion.34
  194.6 2.4 %fusion.35 = f32[1,512,128]{2,1,0:T(8,128)S(1)} fusion(f32[512,3584]{1,0:T(8,128)S(1)} %get-tuple-element.118, f32[512]{0:T(512)S(1)} %get-tuple-element.119, bf16[3584,640]{1,0:T(8,128)(2,1)} %get-tuple-element.148, s32[]{:T(128)S(6)} %select_n.26, f32[512]{0:T(512)S(1)} %fusion.34), kind=kOutput, calls=%fused_computation.8.clone.1 | convolution fusion | flops 473497600 | bytes 8523780 | tf_op jit(solution)/shard_map/while/body/eval_jaxpr/dot_general | solution.py:87
  197.2 0.7 constant_dynamic-update-slice_fusion.8
  197.9 0.6 dynamic_slice.30
  199.2 2.5 %fusion.33 = (f32[512]{0:T(512)S(1)}, f32[512,3584]{1,0:T(8,128)S(1)}) fusion(f32[3584]{0:T(1024)S(1)} %get-tuple-element.147, bf16[3584,640]{1,0:T(8,128)(2,1)} %get-tuple-element.146, s32[]{:T(128)S(6)} %select_n.26, bf16[512,640]{1,0:T(8,128)(2,1)S(1)} %get-tuple-element.145), kind=kOutput, calls=%fused_computation.55.clone.1 | convolution fusion | flops 475266560 | bytes 8408064 | tf_op jit(solution)/shard_map/while/body/eval_jaxpr/dot_general | solution.py:78
  201.6 1.1 fusion.34
  202.8 2.4 %fusion.35 = f32[1,512,128]{2,1,0:T(8,128)S(1)} fusion(f32[512,3584]{1,0:T(8,128)S(1)} %get-tuple-element.118, f32[512]{0:T(512)S(1)} %get-tuple-element.119, bf16[3584,640]{1,0:T(8,128)(2,1)} %get-tuple-element.148, s32[]{:T(128)S(6)} %select_n.26, f32[512]{0:T(512)S(1)} %fusion.34), kind=kOutput, calls=%fused_computation.8.clone.1 | convolution fusion | flops 473497600 | bytes 8523780 | tf_op jit(solution)/shard_map/while/body/eval_jaxpr/dot_general | solution.py:87
  205.3 0.7 constant_dynamic-update-slice_fusion.8
  206.1 0.6 dynamic_slice.30
  207.3 2.5 %fusion.33 = (f32[512]{0:T(512)S(1)}, f32[512,3584]{1,0:T(8,128)S(1)}) fusion(f32[3584]{0:T(1024)S(1)} %get-tuple-element.147, bf16[3584,640]{1,0:T(8,128)(2,1)} %get-tuple-element.146, s32[]{:T(128)S(6)} %select_n.26, bf16[512,640]{1,0:T(8,128)(2,1)S(1)} %get-tuple-element.145), kind=kOutput, calls=%fused_computation.55.clone.1 | convolution fusion | flops 475266560 | bytes 8408064 | tf_op jit(solution)/shard_map/while/body/eval_jaxpr/dot_general | solution.py:78
  209.8 1.1 fusion.34
  210.9 2.4 %fusion.35 = f32[1,512,128]{2,1,0:T(8,128)S(1)} fusion(f32[512,3584]{1,0:T(8,128)S(1)} %get-tuple-element.118, f32[512]{0:T(512)S(1)} %get-tuple-element.119, bf16[3584,640]{1,0:T(8,128)(2,1)} %get-tuple-element.148, s32[]{:T(128)S(6)} %select_n.26, f32[512]{0:T(512)S(1)} %fusion.34), kind=kOutput, calls=%fused_computation.8.clone.1 | convolution fusion | flops 473497600 | bytes 8523780 | tf_op jit(solution)/shard_map/while/body/eval_jaxpr/dot_general | solution.py:87
  213.5 0.7 constant_dynamic-update-slice_fusion.8
  214.2 2.8 %copy.25 = f32[512,640]{1,0:T(8,128)} copy(f32[512,640]{0,1:T(8,128)} %bitcast.46) | data formatting | bytes 2621440 | tf_op jit(solution)/shard_map/reshape | solution.py:93
  (56 shorter events, 2.6 us)
Async XLA Ops:
  0.0 13.3 %copy-start.4 = (bf16[512,640]{1,0:T(8,128)(2,1)S(1)}, bf16[512,640]{1,0:T(8,128)(2,1)}, u32[]{:S(2)}) copy-start(bf16[512,640]{1,0:T(8,128)(2,1)} %param.9) | copy-start | bytes 1966084
  0.0 2.7 %copy-start.9 = (s32[1,16]{1,0:T(1,128)S(1)}, s32[1,16]{1,0:T(1,128)}, u32[]{:S(2)}) copy-start(s32[1,16]{1,0:T(1,128)} %param.13) | copy-start | bytes 196
  0.0 13.3 %copy-start.7 = (f32[640]{0:T(1024)S(1)}, f32[640]{0:T(1024)}, u32[]{:S(2)}) copy-start(f32[640]{0:T(1024)} %param.12) | copy-start | bytes 7684
  0.0 13.5 %copy-start.6 = (bf16[512,640]{1,0:T(8,128)(2,1)S(1)}, bf16[512,640]{1,0:T(8,128)(2,1)}, u32[]{:S(2)}) copy-start(bf16[512,640]{1,0:T(8,128)(2,1)} %param.10) | copy-start | bytes 1966084
  14.6 35.5 %collective-permute-start = (bf16[2,1,512,640]{3,2,0,1:T(8,128)(2,1)S(1)}, bf16[2,1,512,640]{3,2,0,1:T(8,128)(2,1)S(1)}, u32[]{:S(2)}, u32[]{:S(2)}) collective-permute-start(bf16[2,1,512,640]{3,2,0,1:T(8,128)(2,1)S(1)} %bitcast.35), channel_id=1, source_target_pairs={{1,0},{2,1},{3,2},{4,3},{5,4},{6,5},{7,6},{8,7},{9,8},{10,9},{11,1... | collective-permute-start | bytes 3932168 | tf_op jit(solution)/shard_map/ppermute | solution.py:16
  21.2 36.8 %collective-permute-start.1 = (bf16[2,1,512,640]{3,2,0,1:T(8,128)(2,1)S(1)}, bf16[2,1,512,640]{3,2,0,1:T(8,128)(2,1)S(1)}, u32[]{:S(2)}, u32[]{:S(2)}) collective-permute-start(bf16[2,1,512,640]{3,2,0,1:T(8,128)(2,1)S(1)} %bitcast.36), channel_id=1, source_target_pairs={{0,1},{1,2},{2,3},{3,4},{4,5},{5,6},{6,7},{7,8},{8,9},{9,10},{10,1... | collective-permute-start | bytes 3932168 | tf_op jit(solution)/shard_map/ppermute | solution.py:16
  50.1 19.8 %copy-start = (bf16[2,1,512,640]{3,2,0,1:T(8,128)(2,1)}, bf16[2,1,512,640]{3,2,0,1:T(8,128)(2,1)S(1)}, u32[]{:S(2)}) copy-start(bf16[2,1,512,640]{3,2,0,1:T(8,128)(2,1)S(1)} %collective-permute-done) | copy-start | bytes 3932164
  58.0 1.1 copy-start.2
  60.8 62.5 %collective-permute-start.2 = (bf16[2,2,256,640]{3,2,0,1:T(8,128)(2,1)}, bf16[2,2,256,640]{3,2,0,1:T(8,128)(2,1)}, u32[]{:S(2)}, u32[]{:S(2)}) collective-permute-start(bf16[2,2,256,640]{3,2,0,1:T(8,128)(2,1)} %get-tuple-element.64), channel_id=1, source_target_pairs={{2,0},{3,1},{4,2},{5,3},{6,4},{7,5},{8,6},{9,7},{10,8},{11,9},{12,... | collective-permute-start | bytes 3932168 | tf_op jit(solution)/shard_map/ppermute | solution.py:16
  62.8 61.7 %collective-permute-start.3 = (bf16[2,2,256,640]{3,2,0,1:T(8,128)(2,1)}, bf16[2,2,256,640]{3,2,0,1:T(8,128)(2,1)}, u32[]{:S(2)}, u32[]{:S(2)}) collective-permute-start(bf16[2,2,256,640]{3,2,0,1:T(8,128)(2,1)} %get-tuple-element.63), channel_id=1, source_target_pairs={{0,2},{1,3},{2,4},{3,5},{4,6},{5,7},{6,8},{7,9},{8,10},{9,11},{10,... | collective-permute-start | bytes 3932168 | tf_op jit(solution)/shard_map/ppermute | solution.py:16
  69.9 55.7 %slice-start = ((bf16[2,1,512,640]{3,2,0,1:T(8,128)(2,1)}), bf16[2,1,128,640]{3,2,0,1:T(8,128)(2,1)S(1)}, s32[]{:S(2)}) async-start(bf16[2,1,512,640]{3,2,0,1:T(8,128)(2,1)} %copy-done), calls=%async_computation | async-start | bytes 655360 | tf_op jit(solution)/shard_map/slice | solution.py:28
  70.0 55.7 %slice-start.1 = ((bf16[2,1,512,640]{3,2,0,1:T(8,128)(2,1)}), bf16[2,1,128,640]{3,2,0,1:T(8,128)(2,1)S(1)}, s32[]{:S(2)}) async-start(bf16[2,1,512,640]{3,2,0,1:T(8,128)(2,1)} %copy-done.2), calls=%async_computation.1 | async-start | bytes 655360 | tf_op jit(solution)/shard_map/slice | solution.py:28
  127.5 32.1 %collective-permute-start.4 = (bf16[2,4,128,640]{3,2,0,1:T(8,128)(2,1)}, bf16[2,4,128,640]{3,2,0,1:T(8,128)(2,1)}, u32[]{:S(2)}, u32[]{:S(2)}) collective-permute-start(bf16[2,4,128,640]{3,2,0,1:T(8,128)(2,1)} %get-tuple-element.66), channel_id=1, source_target_pairs={{4,0},{5,1},{6,2},{7,3},{8,4},{9,5},{10,6},{11,7},{12,8},{13,9},{1... | collective-permute-start | bytes 3932168 | tf_op jit(solution)/shard_map/ppermute | solution.py:16
  129.4 33.3 %collective-permute-start.5 = (bf16[2,4,128,640]{3,2,0,1:T(8,128)(2,1)}, bf16[2,4,128,640]{3,2,0,1:T(8,128)(2,1)}, u32[]{:S(2)}, u32[]{:S(2)}) collective-permute-start(bf16[2,4,128,640]{3,2,0,1:T(8,128)(2,1)} %get-tuple-element.65), channel_id=1, source_target_pairs={{0,4},{1,5},{2,6},{3,7},{4,8},{5,9},{6,10},{7,11},{8,12},{9,13},{1... | collective-permute-start | bytes 3932168 | tf_op jit(solution)/shard_map/ppermute | solution.py:16
  133.4 1.2 copy-start.5
  133.4 1.2 copy-start.8
  134.6 1.3 copy-start.1
  135.9 1.8 copy-start.3
where the time goes:
time: 218 us; the launch traced here: 217 us
  waiting for transfers between devices  104 us (48%)
  local copies, waits for them, and re-layouts  40 us (18%)
  matrix products  24.4 us (11%)
  starting transfers between devices  21.7 us (10%)
  other arithmetic  12.6 us (6%)
  blocking collectives  10.5 us (5%)
  loops' own time  3.36 us (2%)
    ppermute x6, waiting for transfers between devices, from_behind(): lax.ppermute(value, axis, [(source, source + steps) for source in range(i...  104 us
    ppermute x6, starting transfers between devices, from_behind(): lax.ppermute(value, axis, [(source, source + steps) for source in range(i...  21.7 us
    dot_general x5, matrix products, attend_head(): lax.dot_general(query_head, key_head, (((1,), (1,)), ((), ())), preferred...  12.3 us
    dot_general x5, matrix products, attend_head(): jnp.dot(weights.astype(jnp.bfloat16), value_head, preferred_element_type=...  12.1 us
    unnamed x32, local copies, waits for them, and re-layouts  11.2 us
    psum x1, blocking collectives, on_device(): lax.psum((jnp.sum(query_float * query_float, axis=1), jnp.sum(key_float *...  10.5 us
    squeeze x1, local copies, waits for them, and re-layouts, on_device(): joined_values = joined[1]  8.05 us
    ppermute x4, local copies, waits for them, and re-layouts, from_behind(): lax.ppermute(value, axis, [(source, source + steps) for source in range(i...  5.72 us
  transfers between devices with their start and end apart: 6, of which 5 were waited for; matrix products, arithmetic and copies ran while one was open for 7% of the time, Pallas kernels for 0%

commit v1 on v0

v1 whole, which is shorter than its diff:
```python
import functools
import math

import jax
import jax.numpy as jnp
from jax import lax
from jax.experimental import pallas as pl
from jax.experimental.pallas import tpu as pltpu
from jax.sharding import PartitionSpec as P

HD = 128
EPS = 1e-06
LOG2E = math.log2(math.e)
VMEM_LIMIT = 48 << 20
FAR = 1e30


def shift(value, steps):
    count = lax.axis_size("frames")
    initial, last = (max(0, -steps), min(count, count - steps))
    return lax.ppermute(
        value, "frames", [(source, source + steps) for source in range(initial, last)]
    )


def row_squares(value):
    wide = value.astype(jnp.float32)
    wide = wide * wide
    folded = wide[:, :HD]
    for start in range(HD, value.shape[1], HD):
        folded = folded + wide[:, start : start + HD]
    return jnp.sum(folded.T, axis=0, keepdims=True)


def gather_kernel(blocks_ref, query_ref, key_ref, value_ref, ranked_ref, squares_ref):
    block_count = blocks_ref.shape[1]
    size = value_ref.shape[0] // block_count
    for rank in range(block_count):
        start = pl.multiple_of(blocks_ref[0, rank] * size, size)
        ranked_ref[rank * size : (rank + 1) * size, :] = value_ref[pl.ds(start, size), :]
    squares_ref[0:1, :] = row_squares(query_ref[...])
    squares_ref[1:2, :] = row_squares(key_ref[...])


def norm_kernel(
    width_total,
    blocks_ref,
    squares_ref,
    query_ref,
    key_ref,
    ranked_value_ref,
    query_gain_ref,
    key_gain_ref,
    query_out_ref,
    key_out_ref,
    half_ref,
    plain_ref,
):
    rows, width = query_ref.shape
    factors = lax.rsqrt(squares_ref[...] / width_total + EPS)
    query_factor = jnp.broadcast_to(factors[0:1, :], (HD, rows)).T
    key_factor = jnp.broadcast_to(factors[1:2, :], (HD, rows)).T
    for start in range(0, width, HD):
        lanes = slice(start, start + HD)
        query = query_ref[:, lanes].astype(jnp.float32)
        query_out_ref[:, lanes] = (query * query_factor * query_gain_ref[:, lanes]).astype(
            jnp.bfloat16
        )
        key = key_ref[:, lanes].astype(jnp.float32)
        plain_ref[:, lanes] = (key * key_factor * key_gain_ref[:, lanes]).astype(jnp.bfloat16)
    block_count = blocks_ref.shape[1]
    size = rows // block_count
    for rank in range(block_count):
        start = pl.multiple_of(blocks_ref[0, rank] * size, size)
        key_out_ref[rank * size : (rank + 1) * size, :] = plain_ref[pl.ds(start, size), :]
    half = rows // 2
    half_ref[:half, :] = key_out_ref[:half, :]
    half_ref[half:, :] = ranked_value_ref[:half, :]


def attend_kernel(pieces, first, last, operand_count, valid_ref, query_ref, *refs):
    operands = refs[:operand_count]
    rest = refs[operand_count:]
    if not first:
        old_mixed_ref, old_stats_ref = rest[:2]
        rest = rest[2:]
    rows, width = query_ref.shape
    scale = HD ** (-0.5) * LOG2E
    for head in range(width // HD):
        lanes = slice(head * HD, (head + 1) * HD)
        query = query_ref[:, lanes]
        tops = []
        scores = []
        for key_at, key_start, _, _, count, flag in pieces:
            key = operands[key_at][key_start : key_start + count, lanes]
            score = lax.dot_general(
                key, query, (((1,), (1,)), ((), ())), preferred_element_type=jnp.float32
            )
            top = jnp.max(score, axis=0, keepdims=True) * scale
            if flag is not None:
                top = jnp.where(valid_ref[flag] > 0, top, -FAR)
            scores.append(score)
            tops.append(top)
        top = functools.reduce(jnp.maximum, tops)
        if not first:
            old_top = old_stats_ref[head : head + 1, :]
            top = jnp.maximum(top, old_top)
            keep = jnp.exp2(old_top - top)
        total = None
        weights = []
        values = []
        for score, (_, _, value_at, value_start, count, flag) in zip(scores, pieces):
            level = top if flag is None else jnp.where(valid_ref[flag] > 0, top, FAR)
            weight = jnp.exp2(score * scale - level)
            part = jnp.sum(weight, axis=0, keepdims=True)
            total = part if total is None else total + part
            weights.append(weight.astype(jnp.bfloat16))
            values.append(operands[value_at][value_start : value_start + count, lanes])
        weights = weights[0] if len(weights) == 1 else jnp.concatenate(weights, axis=0)
        values = values[0] if len(values) == 1 else jnp.concatenate(values, axis=0)
        mixed = lax.dot_general(
            values, weights, (((0,), (0,)), ((), ())), preferred_element_type=jnp.float32
        )
        if not first:
            mixed = mixed + keep * old_mixed_ref[head * HD : (head + 1) * HD, :]
            total = total + keep * old_stats_ref[8 + head : 9 + head, :]
        if last:
            rest[0][:, lanes] = (mixed / total).T
        else:
            rest[0][head * HD : (head + 1) * HD, :] = mixed
            rest[1][head : head + 1, :] = top
            rest[1][8 + head : 9 + head, :] = total


def attend(query, operands, pieces, valid, state=None, last=False):
    rows, width = query.shape
    heads = width // HD
    keys = sum(piece[4] for piece in pieces)
    first = state is None
    mixed = jax.ShapeDtypeStruct((width, rows), jnp.float32)
    stats = jax.ShapeDtypeStruct((16, rows), jnp.float32)
    out = jax.ShapeDtypeStruct((rows, width), jnp.float32)
    inputs = [valid, query, *operands] + ([] if first else list(state))
    vmem = pl.BlockSpec(memory_space=pltpu.VMEM)
    aliases = {}
    if not first and not last:
        aliases = {len(inputs) - 2: 0, len(inputs) - 1: 1}
    moved = 2 * (query.size + sum(operand.size for operand in operands)) + 8 * rows * width
    return pl.pallas_call(
        functools.partial(attend_kernel, pieces, first, last, len(operands)),
        out_shape=out if last else (mixed, stats),
        in_specs=[pl.BlockSpec(memory_space=pltpu.SMEM)] + [vmem] * (len(inputs) - 1),
        out_specs=vmem if last else (vmem, vmem),
        input_output_aliases=aliases,
        compiler_params=pltpu.CompilerParams(vmem_limit_bytes=VMEM_LIMIT),
        cost_estimate=pl.CostEstimate(
            flops=4 * rows * keys * width,
            bytes_accessed=moved,
            transcendentals=rows * keys * heads,
        ),
    )(*inputs)


def on_device(query_proj, key_proj, value_proj, query_gain, key_gain, key_blocks):
    rows, width = query_proj.shape
    width_total = width * lax.axis_size("heads")
    frame_count = lax.axis_size("frames")
    frame = lax.axis_index("frames")
    half, quarter = rows // 2, rows // 4
    smem = pl.BlockSpec(memory_space=pltpu.SMEM)
    vmem = pl.BlockSpec(memory_space=pltpu.VMEM)
    params = pltpu.CompilerParams(vmem_limit_bytes=VMEM_LIMIT)
    block = jax.ShapeDtypeStruct((rows, width), jnp.bfloat16)

    own_value, squares = pl.pallas_call(
        gather_kernel,
        out_shape=(block, jax.ShapeDtypeStruct((2, rows), jnp.float32)),
        in_specs=[smem, vmem, vmem, vmem],
        out_specs=(vmem, vmem),
        compiler_params=params,
        cost_estimate=pl.CostEstimate(flops=4 * rows * width, bytes_accessed=8 * rows * width, transcendentals=0),
    )(key_blocks, query_proj, key_proj, value_proj)
    near_value = [shift(own_value, step) for step in (1, -1)]
    squares = lax.psum(squares, "heads")
    query, own_key, own_half = pl.pallas_call(
        functools.partial(norm_kernel, width_total),
        out_shape=(block, block, block),
        in_specs=[smem] + [vmem] * 6,
        out_specs=(vmem, vmem, vmem),
        scratch_shapes=[pltpu.VMEM((rows, width), jnp.bfloat16)],
        compiler_params=params,
        cost_estimate=pl.CostEstimate(flops=6 * rows * width, bytes_accessed=12 * rows * width, transcendentals=0),
    )(
        key_blocks,
        squares,
        query_proj,
        key_proj,
        own_value,
        query_gain.reshape(1, width),
        key_gain.reshape(1, width),
    )
    near_key = [shift(own_key, step) for step in (1, -1)]
    third = [shift(own_half, 3 * step) for step in (1, -1)]
    relayed = [jnp.concatenate([key[:half], value[:half]]) for key, value in zip(near_key, near_value)]
    second = [shift(value, step) for value, step in zip(relayed, (1, -1))]
    far = [
        shift(
            jnp.concatenate(
                [
                    own_key[:quarter],
                    near_key[side][:quarter],
                    third[side][:quarter],
                    own_value[:quarter],
                    near_value[side][:quarter],
                    third[side][half : half + quarter],
                ]
            ),
            4 * step,
        )
        for side, step in enumerate((1, -1))
    ]
    sixth = [
        shift(jnp.concatenate([second[side][:quarter], second[side][half : half + quarter]]), 4 * step)
        for side, step in enumerate((1, -1))
    ]

    distance = jnp.arange(1, 8, dtype=jnp.int32)
    valid = jnp.concatenate([frame - distance >= 0, frame + distance < frame_count]).astype(jnp.int32)

    def flag(side, steps):
        return side * 7 + steps - 1

    state = attend(query, [own_key, own_value], [(0, 0, 1, 0, rows, None)], valid)
    state = attend(
        query,
        [*near_key, *near_value],
        [(side, 0, 2 + side, 0, rows, flag(side, 1)) for side in range(2)],
        valid,
        state,
    )
    state = attend(
        query, third, [(side, 0, side, half, half, flag(side, 3)) for side in range(2)], valid, state
    )
    state = attend(
        query, second, [(side, 0, side, half, half, flag(side, 2)) for side in range(2)], valid, state
    )
    state = attend(
        query,
        far,
        [
            (side, place * quarter, side, (3 + place) * quarter, quarter, flag(side, steps))
            for side in range(2)
            for place, steps in enumerate((4, 5, 7))
        ],
        valid,
        state,
    )
    return attend(
        query,
        sixth,
        [(side, 0, side, quarter, quarter, flag(side, 6)) for side in range(2)],
        valid,
        state,
        last=True,
    )


def solution(mesh):
    placed = (
        P("frames", "heads"),
        P("frames", "heads"),
        P("frames", "heads"),
        P("heads"),
        P("heads"),
        P("frames", None),
    )
    return jax.shard_map(
        on_device, mesh=mesh, in_specs=placed, out_specs=P("frames", "heads"), check_vma=False
    )
```

time: 218 us -> 126 us (0.58)
  the two profiles are of different devices: /device:TPU:390 before, /device:TPU:414 now
where the time goes in v1:
time: 126 us; the launch traced here: 125 us
  starting transfers between devices  49.7 us (39%)
  Pallas kernels  29 us (23%)
  waiting for transfers between devices  26 us (21%)
  blocking collectives  10.5 us (8%)
  local copies, waits for them, and re-layouts  9.07 us (7%)
    ppermute x12, starting transfers between devices, shift(): lax.ppermute(value, 'frames', [(source, source + steps) for source in ran...  49.7 us
    pallas_call x6, Pallas kernels, attend(): pl.pallas_call(functools.partial(attend_kernel, pieces, first, last, len(...  26 us
    ppermute x12, waiting for transfers between devices, shift(): lax.ppermute(value, 'frames', [(source, source + steps) for source in ran...  26 us
    psum x1, blocking collectives, on_device(): squares = lax.psum(squares, 'heads')  10.5 us
    unnamed x32, local copies, waits for them, and re-layouts  6.9 us
  transfers between devices with their start and end apart: 12, of which 5 were waited for; matrix products, arithmetic and copies ran while one was open for 4% of the time, Pallas kernels for 18%

profile of v1, /device:TPU:414, one launch (start us, length us, event | category | flops | bytes accessed | tf_op | source)
XLA Modules:
  0.0 125.0 jit_solution(15197056956768125974)
XLA Ops:
  0.0 0.0 copy-start
  0.0 1.1 copy-done
  1.1 0.0 copy-start.2
  1.1 1.1 copy-done.2
  2.2 0.0 copy-start.4
  2.2 1.1 copy-done.4
  3.3 0.0 copy-start.5
  3.3 0.7 copy-done.5
  3.9 0.0 copy-start.10
  3.9 0.0 copy-start.11
  3.9 0.0 copy-start.1
  3.9 0.0 copy-start.6
  3.9 0.9 shard_map.64
  4.8 10.5 %psum.7.squares_ref = f32[2,512]{1,0:T(2,128)S(1)} all-reduce(f32[2,512]{1,0:T(2,128)S(1)} %get-tuple-element.20), channel_id=1, replica_groups=mesh['heads'=8,'frames'=64] {'heads'}, use_global_device_ids=true, to_apply=%region_0.0 | all-reduce | flops 1024 | bytes 8192 | tf_op jit(solution)/shard_map/psum | solution.py:184
  15.4 0.0 copy-done.10
  15.4 0.0 copy-done.11
  15.4 0.0 copy-done.1
  15.4 0.0 copy-done.3
  15.4 0.0 copy-done.6
  15.4 2.1 %shard_map.65 = (bf16[512,640]{1,0:T(8,128)(2,1)S(1)}, bf16[512,640]{1,0:T(8,128)(2,1)}, bf16[512,640]{1,0:T(8,128)(2,1)}) custom-call(s32[1,16]{1,0:T(1,128)S(1)} %copy-done.6, f32[2,512]{1,0:T(2,128)S(1)} %psum.7.squares_ref, bf16[512,640]{1,0:T(8,128)(2,1)S(1)} %copy-done.1, bf16[512,640]{1,0:T(8,128)(2,1)S(1)} %copy-done.3, ...), custom_call_target="tpu_custom_call" | custom-call | flops 1966080 | bytes 3932160 | tf_op jit(solution)/shard_map/pallas_call | solution.py:185
  17.5 2.6 %collective-permute-start.4 = (bf16[512,640]{1,0:T(8,128)(2,1)}, bf16[512,640]{1,0:T(8,128)(2,1)S(1)}, u32[]{:S(2)}, u32[]{:S(2)}) collective-permute-start(bf16[512,640]{1,0:T(8,128)(2,1)} %get-tuple-element.23.refs_0_), channel_id=1, source_target_pairs={{1,0},{2,1},{3,2},{4,3},{5,4},{6,5},{7,6},{8,7},{9,8},{10,9},{11,1... | collective-permute-start | bytes 1966088 | tf_op jit(solution)/shard_map/ppermute | solution.py:21
  20.2 2.4 %collective-permute-start.5 = (bf16[512,640]{1,0:T(8,128)(2,1)S(1)}, bf16[512,640]{1,0:T(8,128)(2,1)S(1)}, u32[]{:S(2)}, u32[]{:S(2)}) collective-permute-start(bf16[512,640]{1,0:T(8,128)(2,1)S(1)} %get-tuple-element.21.ranked_value_ref.refs_1_), channel_id=1, source_target_pairs={{1,0},{2,1},{3,2},{4,3},{5,4},{6,5},{7,6},{8,7},{9,8},{10,9},{11,1... | collective-permute-start | bytes 1966088 | tf_op jit(solution)/shard_map/ppermute | solution.py:21
  22.5 5.6 %collective-permute-start = (bf16[512,640]{1,0:T(8,128)(2,1)}, bf16[512,640]{1,0:T(8,128)(2,1)}, u32[]{:S(2)}, u32[]{:S(2)}) collective-permute-start(bf16[512,640]{1,0:T(8,128)(2,1)} %get-tuple-element.23.refs_0_), channel_id=1, source_target_pairs={{0,1},{1,2},{2,3},{3,4},{4,5},{5,6},{6,7},{7,8},{8,9},{9,10},{10,1... | collective-permute-start | bytes 1966088 | tf_op jit(solution)/shard_map/ppermute | solution.py:21
  28.1 3.2 %collective-permute-start.1 = (bf16[512,640]{1,0:T(8,128)(2,1)S(1)}, bf16[512,640]{1,0:T(8,128)(2,1)}, u32[]{:S(2)}, u32[]{:S(2)}) collective-permute-start(bf16[512,640]{1,0:T(8,128)(2,1)S(1)} %get-tuple-element.21.ranked_value_ref.refs_1_), channel_id=1, source_target_pairs={{0,1},{1,2},{2,3},{3,4},{4,5},{5,6},{6,7},{7,8},{8,9},{9,10},{10,1... | collective-permute-start | bytes 1966088 | tf_op jit(solution)/shard_map/ppermute | solution.py:21
  31.4 2.7 %collective-permute-start.10 = (bf16[512,640]{1,0:T(8,128)(2,1)}, bf16[512,640]{1,0:T(8,128)(2,1)S(1)}, u32[]{:S(2)}, u32[]{:S(2)}) collective-permute-start(bf16[512,640]{1,0:T(8,128)(2,1)} %get-tuple-element.24), channel_id=1, source_target_pairs={{3,0},{4,1},{5,2},{6,3},{7,4},{8,5},{9,6},{10,7},{11,8},{12,9},{13... | collective-permute-start | bytes 1966088 | tf_op jit(solution)/shard_map/ppermute | solution.py:21
  34.0 0.9 slice_dynamic-update-slice_fusion.11
  35.0 0.0 copy-start.7
  35.0 0.1 add_convert_fusion.valid_ref
  35.1 4.1 %collective-permute-done.4.refs_1_ = bf16[512,640]{1,0:T(8,128)(2,1)S(1)} collective-permute-done((bf16[512,640]{1,0:T(8,128)(2,1)}, bf16[512,640]{1,0:T(8,128)(2,1)S(1)}, u32[]{:S(2)}, u32[]{:S(2)}) %collective-permute-start.4) | collective-permute-done | bytes 655392 | tf_op jit(solution)/shard_map/ppermute | solution.py:21
  39.1 1.9 %collective-permute-start.8 = (bf16[512,640]{1,0:T(8,128)(2,1)}, bf16[512,640]{1,0:T(8,128)(2,1)S(1)}, u32[]{:S(2)}, u32[]{:S(2)}) collective-permute-start(bf16[512,640]{1,0:T(8,128)(2,1)} %get-tuple-element.24), channel_id=1, source_target_pairs={{0,3},{1,4},{2,5},{3,6},{4,7},{5,8},{6,9},{7,10},{8,11},{9,12},{10... | collective-permute-start | bytes 1966088 | tf_op jit(solution)/shard_map/ppermute | solution.py:21
  41.1 0.0 copy-done.7
  41.1 12.2 %collective-permute-done.5.refs_3_ = bf16[512,640]{1,0:T(8,128)(2,1)S(1)} collective-permute-done((bf16[512,640]{1,0:T(8,128)(2,1)S(1)}, bf16[512,640]{1,0:T(8,128)(2,1)S(1)}, u32[]{:S(2)}, u32[]{:S(2)}) %collective-permute-start.5) | collective-permute-done | bytes 655392 | tf_op jit(solution)/shard_map/ppermute | solution.py:21
  53.3 0.1 pad_maximum_fusion.1
  53.4 0.0 copy-start.9
  53.4 12.6 %collective-permute-start.6 = (bf16[512,640]{1,0:T(8,128)(2,1)S(1)}, bf16[512,640]{1,0:T(8,128)(2,1)S(1)}, u32[]{:S(2)}, u32[]{:S(2)}) collective-permute-start(bf16[512,640]{1,0:T(8,128)(2,1)S(1)} %pad_maximum_fusion.1), channel_id=1, source_target_pairs={{1,0},{2,1},{3,2},{4,3},{5,4},{6,5},{7,6},{8,7},{9,8},{10,9},{11,1... | collective-permute-start | bytes 1966088 | tf_op jit(solution)/shard_map/ppermute | solution.py:21
  66.0 0.0 collective-permute-done.refs_0_
  66.0 1.0 slice.74
  67.0 0.0 copy-start.8
  67.0 3.1 %collective-permute-done.1.refs_2_ = bf16[512,640]{1,0:T(8,128)(2,1)} collective-permute-done((bf16[512,640]{1,0:T(8,128)(2,1)S(1)}, bf16[512,640]{1,0:T(8,128)(2,1)}, u32[]{:S(2)}, u32[]{:S(2)}) %collective-permute-start.1) | collective-permute-done | bytes 655392 | tf_op jit(solution)/shard_map/ppermute | solution.py:21
  70.1 1.0 slice.75
  71.1 0.1 pad_maximum_fusion
  71.2 4.3 %collective-permute-start.2 = (bf16[512,640]{1,0:T(8,128)(2,1)S(1)}, bf16[512,640]{1,0:T(8,128)(2,1)S(1)}, u32[]{:S(2)}, u32[]{:S(2)}) collective-permute-start(bf16[512,640]{1,0:T(8,128)(2,1)S(1)} %pad_maximum_fusion), channel_id=1, source_target_pairs={{0,1},{1,2},{2,3},{3,4},{4,5},{5,6},{6,7},{7,8},{8,9},{9,10},{10,1... | collective-permute-start | bytes 1966088 | tf_op jit(solution)/shard_map/ppermute | solution.py:21
  75.5 0.0 copy-done.9
  75.5 0.9 slice_dynamic-update-slice_fusion.7
  76.4 0.0 copy-done.8
  76.5 0.0 collective-permute-done.8.refs_0_
  76.5 0.0 collective-permute-done.10.refs_1_
  76.6 5.3 %collective-permute-start.11 = (bf16[768,640]{1,0:T(8,128)(2,1)S(1)}, bf16[768,640]{1,0:T(8,128)(2,1)S(1)}, u32[]{:S(2)}, u32[]{:S(2)}) collective-permute-start(bf16[768,640]{1,0:T(8,128)(2,1)S(1)} %slice_dynamic-update-slice_fusion), channel_id=1, source_target_pairs={{4,0},{5,1},{6,2},{7,3},{8,4},{9,5},{10,6},{11,7},{12,8},{13,9},{1... | collective-permute-start | bytes 2949128 | tf_op jit(solution)/shard_map/ppermute | solution.py:21
  82.0 0.9 slice_dynamic-update-slice_fusion.5
  83.0 1.9 %collective-permute-start.9 = (bf16[768,640]{1,0:T(8,128)(2,1)S(1)}, bf16[768,640]{1,0:T(8,128)(2,1)S(1)}, u32[]{:S(2)}, u32[]{:S(2)}) collective-permute-start(bf16[768,640]{1,0:T(8,128)(2,1)S(1)} %slice_dynamic-update-slice_fusion.4), channel_id=1, source_target_pairs={{0,4},{1,5},{2,6},{3,7},{4,8},{5,9},{6,10},{7,11},{8,12},{9,13},{1... | collective-permute-start | bytes 2949128 | tf_op jit(solution)/shard_map/ppermute | solution.py:21
  84.9 3.9 %shard_map.66 = (f32[640,512]{1,0:T(8,128)S(1)}, f32[16,512]{1,0:T(8,128)S(1)}) custom-call(s32[14]{0:T(128)S(1)} %add_convert_fusion.valid_ref, bf16[512,640]{1,0:T(8,128)(2,1)S(1)} %get-tuple-element.22.query_ref, bf16[512,640]{1,0:T(8,128)(2,1)} %get-tuple-element.23.refs_0_, bf16[512,640]{1,0:T(8,128)(2,1)S(1)} %get-tuple-element.21.ranked_value_ref.refs_1_), custom_call_target="tpu_custom_call" | custom-call | flops 671088640 | bytes 4587520 | tf_op jit(solution)/shard_map/pallas_call | solution.py:149
  88.8 0.0 collective-permute-done.6.refs_1_
  88.9 5.1 %collective-permute-start.7 = (bf16[256,640]{1,0:T(8,128)(2,1)S(1)}, bf16[256,640]{1,0:T(8,128)(2,1)S(1)}, u32[]{:S(2)}, u32[]{:S(2)}) collective-permute-start(bf16[256,640]{1,0:T(8,128)(2,1)S(1)} %pad_maximum_fusion.3), channel_id=1, source_target_pairs={{4,0},{5,1},{6,2},{7,3},{8,4},{9,5},{10,6},{11,7},{12,8},{13,9},{1... | collective-permute-start | bytes 983048 | tf_op jit(solution)/shard_map/ppermute | solution.py:21
  94.1 0.0 collective-permute-done.2.refs_0_
  94.1 2.1 %collective-permute-start.3 = (bf16[256,640]{1,0:T(8,128)(2,1)S(1)}, bf16[256,640]{1,0:T(8,128)(2,1)S(1)}, u32[]{:S(2)}, u32[]{:S(2)}) collective-permute-start(bf16[256,640]{1,0:T(8,128)(2,1)S(1)} %pad_maximum_fusion.2), channel_id=1, source_target_pairs={{0,4},{1,5},{2,6},{3,7},{4,8},{5,9},{6,10},{7,11},{8,12},{9,13},{1... | collective-permute-start | bytes 983048 | tf_op jit(solution)/shard_map/ppermute | solution.py:21
  96.2 6.4 %shard_map.67 = (f32[640,512]{1,0:T(8,128)S(1)}, f32[16,512]{1,0:T(8,128)S(1)}) custom-call(s32[14]{0:T(128)S(1)} %add_convert_fusion.valid_ref, bf16[512,640]{1,0:T(8,128)(2,1)S(1)} %get-tuple-element.22.query_ref, bf16[512,640]{1,0:T(8,128)(2,1)} %collective-permute-done.refs_0_, ...), custom_call_target="tpu_custom_call", output_to_operand_aliasing={{0}: (6, {}), {1}: (7, {})} | custom-call | flops 1342177280 | bytes 5898240 | tf_op jit(solution)/shard_map/pallas_call | solution.py:149
  102.6 3.6 %shard_map.68 = (f32[640,512]{1,0:T(8,128)S(1)}, f32[16,512]{1,0:T(8,128)S(1)}) custom-call(s32[14]{0:T(128)S(1)} %add_convert_fusion.valid_ref, bf16[512,640]{1,0:T(8,128)(2,1)S(1)} %get-tuple-element.22.query_ref, bf16[512,640]{1,0:T(8,128)(2,1)S(1)} %collective-permute-done.8.refs_0_, ...), custom_call_target="tpu_custom_call", output_to_operand_aliasing={{0}: (4, {}), {1}: (5, {})} | custom-call | flops 671088640 | bytes 4587520 | tf_op jit(solution)/shard_map/pallas_call | solution.py:149
  106.2 3.6 %shard_map.69 = (f32[640,512]{1,0:T(8,128)S(1)}, f32[16,512]{1,0:T(8,128)S(1)}) custom-call(s32[14]{0:T(128)S(1)} %add_convert_fusion.valid_ref, bf16[512,640]{1,0:T(8,128)(2,1)S(1)} %get-tuple-element.22.query_ref, bf16[512,640]{1,0:T(8,128)(2,1)S(1)} %collective-permute-done.2.refs_0_, ...), custom_call_target="tpu_custom_call", output_to_operand_aliasing={{0}: (4, {}), {1}: (5, {})} | custom-call | flops 671088640 | bytes 4587520 | tf_op jit(solution)/shard_map/pallas_call | solution.py:149
  109.9 0.0 collective-permute-done.11.refs_1_
  109.9 5.7 %collective-permute-done.9.refs_0_ = bf16[768,640]{1,0:T(8,128)(2,1)S(1)} collective-permute-done((bf16[768,640]{1,0:T(8,128)(2,1)S(1)}, bf16[768,640]{1,0:T(8,128)(2,1)S(1)}, u32[]{:S(2)}, u32[]{:S(2)}) %collective-permute-start.9) | collective-permute-done | bytes 983072 | tf_op jit(solution)/shard_map/ppermute | solution.py:21
  115.5 4.9 %shard_map.70 = (f32[640,512]{1,0:T(8,128)S(1)}, f32[16,512]{1,0:T(8,128)S(1)}) custom-call(s32[14]{0:T(128)S(1)} %add_convert_fusion.valid_ref, bf16[512,640]{1,0:T(8,128)(2,1)S(1)} %get-tuple-element.22.query_ref, bf16[768,640]{1,0:T(8,128)(2,1)S(1)} %collective-permute-done.9.refs_0_, ...), custom_call_target="tpu_custom_call", output_to_operand_aliasing={{0}: (4, {}), {1}: (5, {})} | custom-call | flops 1006632960 | bytes 5242880 | tf_op jit(solution)/shard_map/pallas_call | solution.py:149
  120.5 0.0 collective-permute-done.7.refs_1_
  120.5 1.0 collective-permute-done.3.refs_0_
  121.4 3.6 %shard_map.71 = f32[512,640]{1,0:T(8,128)} custom-call(s32[14]{0:T(128)S(1)} %add_convert_fusion.valid_ref, bf16[512,640]{1,0:T(8,128)(2,1)S(1)} %get-tuple-element.22.query_ref, bf16[256,640]{1,0:T(8,128)(2,1)S(1)} %collective-permute-done.3.refs_0_, bf16[256,640]{1,0:T(8,128)(2,1)S(1)} %collective-permute-done.7.refs_1_, ...), custom_call_target="tpu_custom_call" | custom-call | flops 335544320 | bytes 3932160 | tf_op jit(solution)/shard_map/pallas_call | solution.py:149
  (17 shorter events, 0.4 us)
Async XLA Ops:
  0.0 1.1 copy-start
  1.1 1.1 copy-start.2
  2.2 1.1 copy-start.4
  3.3 0.7 copy-start.5
  3.9 11.4 %copy-start.10 = (f32[640]{0:T(1024)S(1)}, f32[640]{0:T(1024)}, u32[]{:S(2)}) copy-start(f32[640]{0:T(1024)} %param.9) | copy-start | bytes 7684
  3.9 11.5 %copy-start.11 = (f32[640]{0:T(1024)S(1)}, f32[640]{0:T(1024)}, u32[]{:S(2)}) copy-start(f32[640]{0:T(1024)} %param.10) | copy-start | bytes 7684
  3.9 11.5 %copy-start.1 = (bf16[512,640]{1,0:T(8,128)(2,1)S(1)}, bf16[512,640]{1,0:T(8,128)(2,1)}, u32[]{:S(2)}) copy-start(bf16[512,640]{1,0:T(8,128)(2,1)} %query_ref.3) | copy-start | bytes 1966084
  3.9 11.5 %copy-start.3 = (bf16[512,640]{1,0:T(8,128)(2,1)S(1)}, bf16[512,640]{1,0:T(8,128)(2,1)}, u32[]{:S(2)}) copy-start(bf16[512,640]{1,0:T(8,128)(2,1)} %key_ref.3) | copy-start | bytes 1966084
  3.9 11.5 %copy-start.6 = (s32[1,16]{1,0:T(1,128)S(1)}, s32[1,16]{1,0:T(1,128)}, u32[]{:S(2)}) copy-start(s32[1,16]{1,0:T(1,128)} %blocks_ref.3) | copy-start | bytes 196
  17.5 21.6 %collective-permute-start.4 = (bf16[512,640]{1,0:T(8,128)(2,1)}, bf16[512,640]{1,0:T(8,128)(2,1)S(1)}, u32[]{:S(2)}, u32[]{:S(2)}) collective-permute-start(bf16[512,640]{1,0:T(8,128)(2,1)} %get-tuple-element.23.refs_0_), channel_id=1, source_target_pairs={{1,0},{2,1},{3,2},{4,3},{5,4},{6,5},{7,6},{8,7},{9,8},{10,9},{11,1... | collective-permute-start | bytes 1966088 | tf_op jit(solution)/shard_map/ppermute | solution.py:21
  20.2 33.1 %collective-permute-start.5 = (bf16[512,640]{1,0:T(8,128)(2,1)S(1)}, bf16[512,640]{1,0:T(8,128)(2,1)S(1)}, u32[]{:S(2)}, u32[]{:S(2)}) collective-permute-start(bf16[512,640]{1,0:T(8,128)(2,1)S(1)} %get-tuple-element.21.ranked_value_ref.refs_1_), channel_id=1, source_target_pairs={{1,0},{2,1},{3,2},{4,3},{5,4},{6,5},{7,6},{8,7},{9,8},{10,9},{11,1... | collective-permute-start | bytes 1966088 | tf_op jit(solution)/shard_map/ppermute | solution.py:21
  22.5 43.4 %collective-permute-start = (bf16[512,640]{1,0:T(8,128)(2,1)}, bf16[512,640]{1,0:T(8,128)(2,1)}, u32[]{:S(2)}, u32[]{:S(2)}) collective-permute-start(bf16[512,640]{1,0:T(8,128)(2,1)} %get-tuple-element.23.refs_0_), channel_id=1, source_target_pairs={{0,1},{1,2},{2,3},{3,4},{4,5},{5,6},{6,7},{7,8},{8,9},{9,10},{10,1... | collective-permute-start | bytes 1966088 | tf_op jit(solution)/shard_map/ppermute | solution.py:21
  28.1 41.9 %collective-permute-start.1 = (bf16[512,640]{1,0:T(8,128)(2,1)S(1)}, bf16[512,640]{1,0:T(8,128)(2,1)}, u32[]{:S(2)}, u32[]{:S(2)}) collective-permute-start(bf16[512,640]{1,0:T(8,128)(2,1)S(1)} %get-tuple-element.21.ranked_value_ref.refs_1_), channel_id=1, source_target_pairs={{0,1},{1,2},{2,3},{3,4},{4,5},{5,6},{6,7},{7,8},{8,9},{9,10},{10,1... | collective-permute-start | bytes 1966088 | tf_op jit(solution)/shard_map/ppermute | solution.py:21
  31.4 45.1 %collective-permute-start.10 = (bf16[512,640]{1,0:T(8,128)(2,1)}, bf16[512,640]{1,0:T(8,128)(2,1)S(1)}, u32[]{:S(2)}, u32[]{:S(2)}) collective-permute-start(bf16[512,640]{1,0:T(8,128)(2,1)} %get-tuple-element.24), channel_id=1, source_target_pairs={{3,0},{4,1},{5,2},{6,3},{7,4},{8,5},{9,6},{10,7},{11,8},{12,9},{13... | collective-permute-start | bytes 1966088 | tf_op jit(solution)/shard_map/ppermute | solution.py:21
  35.0 6.1 %copy-start.7 = (bf16[768,640]{1,0:T(8,128)(2,1)}, bf16[768,640]{1,0:T(8,128)(2,1)S(1)}, u32[]{:S(2)}) copy-start(bf16[768,640]{1,0:T(8,128)(2,1)S(1)} %slice_dynamic-update-slice_fusion.11) | copy-start | bytes 2949124
  39.1 37.3 %collective-permute-start.8 = (bf16[512,640]{1,0:T(8,128)(2,1)}, bf16[512,640]{1,0:T(8,128)(2,1)S(1)}, u32[]{:S(2)}, u32[]{:S(2)}) collective-permute-start(bf16[512,640]{1,0:T(8,128)(2,1)} %get-tuple-element.24), channel_id=1, source_target_pairs={{0,3},{1,4},{2,5},{3,6},{4,7},{5,8},{6,9},{7,10},{8,11},{9,12},{10... | collective-permute-start | bytes 1966088 | tf_op jit(solution)/shard_map/ppermute | solution.py:21
  53.4 22.1 %copy-start.9 = (bf16[768,640]{1,0:T(8,128)(2,1)S(1)}, bf16[768,640]{1,0:T(8,128)(2,1)}, u32[]{:S(2)}) copy-start(bf16[768,640]{1,0:T(8,128)(2,1)} %copy-done.7) | copy-start | bytes 2949124
  53.4 35.4 %collective-permute-start.6 = (bf16[512,640]{1,0:T(8,128)(2,1)S(1)}, bf16[512,640]{1,0:T(8,128)(2,1)S(1)}, u32[]{:S(2)}, u32[]{:S(2)}) collective-permute-start(bf16[512,640]{1,0:T(8,128)(2,1)S(1)} %pad_maximum_fusion.1), channel_id=1, source_target_pairs={{1,0},{2,1},{3,2},{4,3},{5,4},{6,5},{7,6},{8,7},{9,8},{10,9},{11,1... | collective-permute-start | bytes 1966088 | tf_op jit(solution)/shard_map/ppermute | solution.py:21
  67.0 9.4 %copy-start.8 = (bf16[768,640]{1,0:T(8,128)(2,1)S(1)}, bf16[768,640]{1,0:T(8,128)(2,1)}, u32[]{:S(2)}) copy-start(bf16[768,640]{1,0:T(8,128)(2,1)} %copy-done.7) | copy-start | bytes 2949124
  71.2 22.9 %collective-permute-start.2 = (bf16[512,640]{1,0:T(8,128)(2,1)S(1)}, bf16[512,640]{1,0:T(8,128)(2,1)S(1)}, u32[]{:S(2)}, u32[]{:S(2)}) collective-permute-start(bf16[512,640]{1,0:T(8,128)(2,1)S(1)} %pad_maximum_fusion), channel_id=1, source_target_pairs={{0,1},{1,2},{2,3},{3,4},{4,5},{5,6},{6,7},{7,8},{8,9},{9,10},{10,1... | collective-permute-start | bytes 1966088 | tf_op jit(solution)/shard_map/ppermute | solution.py:21
  76.6 33.2 %collective-permute-start.11 = (bf16[768,640]{1,0:T(8,128)(2,1)S(1)}, bf16[768,640]{1,0:T(8,128)(2,1)S(1)}, u32[]{:S(2)}, u32[]{:S(2)}) collective-permute-start(bf16[768,640]{1,0:T(8,128)(2,1)S(1)} %slice_dynamic-update-slice_fusion), channel_id=1, source_target_pairs={{4,0},{5,1},{6,2},{7,3},{8,4},{9,5},{10,6},{11,7},{12,8},{13,9},{1... | collective-permute-start | bytes 2949128 | tf_op jit(solution)/shard_map/ppermute | solution.py:21
  83.0 32.6 %collective-permute-start.9 = (bf16[768,640]{1,0:T(8,128)(2,1)S(1)}, bf16[768,640]{1,0:T(8,128)(2,1)S(1)}, u32[]{:S(2)}, u32[]{:S(2)}) collective-permute-start(bf16[768,640]{1,0:T(8,128)(2,1)S(1)} %slice_dynamic-update-slice_fusion.4), channel_id=1, source_target_pairs={{0,4},{1,5},{2,6},{3,7},{4,8},{5,9},{6,10},{7,11},{8,12},{9,13},{1... | collective-permute-start | bytes 2949128 | tf_op jit(solution)/shard_map/ppermute | solution.py:21
  88.9 31.5 %collective-permute-start.7 = (bf16[256,640]{1,0:T(8,128)(2,1)S(1)}, bf16[256,640]{1,0:T(8,128)(2,1)S(1)}, u32[]{:S(2)}, u32[]{:S(2)}) collective-permute-start(bf16[256,640]{1,0:T(8,128)(2,1)S(1)} %pad_maximum_fusion.3), channel_id=1, source_target_pairs={{4,0},{5,1},{6,2},{7,3},{8,4},{9,5},{10,6},{11,7},{12,8},{13,9},{1... | collective-permute-start | bytes 983048 | tf_op jit(solution)/shard_map/ppermute | solution.py:21
  94.1 27.3 %collective-permute-start.3 = (bf16[256,640]{1,0:T(8,128)(2,1)S(1)}, bf16[256,640]{1,0:T(8,128)(2,1)S(1)}, u32[]{:S(2)}, u32[]{:S(2)}) collective-permute-start(bf16[256,640]{1,0:T(8,128)(2,1)S(1)} %pad_maximum_fusion.2), channel_id=1, source_target_pairs={{0,4},{1,5},{2,6},{3,7},{4,8},{5,9},{6,10},{7,11},{8,12},{9,13},{1... | collective-permute-start | bytes 983048 | tf_op jit(solution)/shard_map/ppermute | solution.py:21

commit v2 on v1

v2 whole, which is shorter than its diff:
```python
import functools
import math

import jax
import jax.numpy as jnp
from jax import lax
from jax.experimental import pallas as pl
from jax.experimental.pallas import tpu as pltpu
from jax.sharding import PartitionSpec as P

HD = 128
EPS = 1e-06
LOG2E = math.log2(math.e)
VMEM_LIMIT = 20 << 20
FAR = 1e30


def shift(value, steps):
    count = lax.axis_size("frames")
    initial, last = (max(0, -steps), min(count, count - steps))
    return lax.ppermute(
        value, "frames", [(source, source + steps) for source in range(initial, last)]
    )


def row_squares(value):
    wide = value.astype(jnp.float32)
    wide = wide * wide
    folded = wide[:, :HD]
    for start in range(HD, value.shape[1], HD):
        folded = folded + wide[:, start : start + HD]
    return jnp.sum(folded.T, axis=0, keepdims=True)


def gather_kernel(
    blocks_ref, query_hbm, key_hbm, value_hbm, ranked_ref, squares_ref, query_ref, key_ref, value_ref, sems
):
    copies = [
        pltpu.make_async_copy(source, target, sems.at[place])
        for place, (source, target) in enumerate(
            ((value_hbm, value_ref), (query_hbm, query_ref), (key_hbm, key_ref))
        )
    ]
    for copy in copies:
        copy.start()
    copies[0].wait()
    block_count = blocks_ref.shape[1]
    size = value_ref.shape[0] // block_count
    for rank in range(block_count):
        start = pl.multiple_of(blocks_ref[0, rank] * size, size)
        ranked_ref[rank * size : (rank + 1) * size, :] = value_ref[pl.ds(start, size), :]
    copies[1].wait()
    query_squares = row_squares(query_ref[...])
    copies[2].wait()
    key_squares = row_squares(key_ref[...])
    for device in range(squares_ref.shape[0]):
        squares_ref[device, 0:1, :] = query_squares
        squares_ref[device, 1:2, :] = key_squares


def norm_kernel(
    width_total,
    blocks_ref,
    squares_ref,
    query_gain_ref,
    key_gain_ref,
    ranked_value_ref,
    query_hbm,
    key_hbm,
    query_out_ref,
    key_out_ref,
    half_ref,
    quarter_ref,
    query_ref,
    key_ref,
    sems,
):
    copies = [
        pltpu.make_async_copy(source, target, sems.at[place])
        for place, (source, target) in enumerate(((key_hbm, key_ref), (query_hbm, query_ref)))
    ]
    for copy in copies:
        copy.start()
    rows, width = query_ref.shape
    squares = squares_ref[0]
    for device in range(1, squares_ref.shape[0]):
        squares = squares + squares_ref[device]
    factors = lax.rsqrt(squares / width_total + EPS)
    query_factor = jnp.broadcast_to(factors[0:1, :], (HD, rows)).T
    key_factor = jnp.broadcast_to(factors[1:2, :], (HD, rows)).T
    copies[0].wait()
    for start in range(0, width, HD):
        lanes = slice(start, start + HD)
        key = key_ref[:, lanes].astype(jnp.float32)
        key_ref[:, lanes] = (key * key_factor * key_gain_ref[:, lanes]).astype(jnp.bfloat16)
    block_count = blocks_ref.shape[1]
    size = rows // block_count
    half, quarter = rows // 2, rows // 4
    for rank in range(block_count):
        start = pl.multiple_of(blocks_ref[0, rank] * size, size)
        block = key_ref[pl.ds(start, size), :]
        at = rank * size
        key_out_ref[at : at + size, :] = block
        if at < half:
            half_ref[at : at + size, :] = block
        if at < quarter:
            quarter_ref[at : at + size, :] = block
    half_ref[half:, :] = ranked_value_ref[:half, :]
    quarter_ref[quarter:, :] = ranked_value_ref[:quarter, :]
    copies[1].wait()
    for start in range(0, width, HD):
        lanes = slice(start, start + HD)
        query = query_ref[:, lanes].astype(jnp.float32)
        query_out_ref[:, lanes] = (query * query_factor * query_gain_ref[:, lanes]).astype(
            jnp.bfloat16
        )


def pack_kernel(parts, *refs):
    sources, (target_ref, sems) = refs[:-2], refs[-2:]
    copies = []
    at = 0
    for place, (source, start, count) in enumerate(parts):
        copies.append(
            pltpu.make_async_copy(
                sources[source].at[pl.ds(start, count), :],
                target_ref.at[pl.ds(at, count), :],
                sems.at[place],
            )
        )
        at += count
    for copy in copies:
        copy.start()
    for copy in copies:
        copy.wait()


def pack(sources, parts):
    width = sources[0].shape[1]
    rows = sum(count for _, _, count in parts)
    anywhere = pl.BlockSpec(memory_space=pl.ANY)
    return pl.pallas_call(
        functools.partial(pack_kernel, parts),
        out_shape=jax.ShapeDtypeStruct((rows, width), jnp.bfloat16),
        in_specs=[anywhere] * len(sources),
        out_specs=anywhere,
        scratch_shapes=[pltpu.SemaphoreType.DMA((len(parts),))],
        compiler_params=pltpu.CompilerParams(vmem_limit_bytes=1 << 20),
        cost_estimate=pl.CostEstimate(flops=0, bytes_accessed=4 * rows * width, transcendentals=0),
    )(*sources)


def attend_kernel(pieces, first, last, operand_count, valid_ref, query_ref, *refs):
    operands = refs[:operand_count]
    rest = refs[operand_count:]
    if not first:
        old_mixed_ref, old_stats_ref = rest[:2]
        rest = rest[2:]
    rows, width = query_ref.shape
    heads = width // HD
    scale = HD ** (-0.5) * LOG2E

    def lanes_of(head):
        return slice(head * HD, (head + 1) * HD)

    def score(head):
        query = query_ref[:, lanes_of(head)]
        return [
            lax.dot_general(
                operands[key_at][start : start + count, lanes_of(head)],
                query,
                (((1,), (1,)), ((), ())),
                preferred_element_type=jnp.float32,
            )
            for key_at, start, _, _, count, _ in pieces
        ]

    def weigh(head, scores):
        tops = []
        for part, (*_, flag) in zip(scores, pieces):
            top = jnp.max(part, axis=0, keepdims=True) * scale
            tops.append(top if flag is None else jnp.where(valid_ref[flag] > 0, top, -FAR))
        top = functools.reduce(jnp.maximum, tops)
        keep = None
        if not first:
            old_top = old_stats_ref[head : head + 1, :]
            top = jnp.maximum(top, old_top)
            keep = jnp.exp2(old_top - top)
        total = None
        weights = []
        for part, (*_, flag) in zip(scores, pieces):
            level = top if flag is None else jnp.where(valid_ref[flag] > 0, top, FAR)
            weight = jnp.exp2(part * scale - level)
            added = jnp.sum(weight, axis=0, keepdims=True)
            total = added if total is None else total + added
            weights.append(weight.astype(jnp.bfloat16))
        weights = weights[0] if len(weights) == 1 else jnp.concatenate(weights, axis=0)
        return top, keep, total, weights

    def mix(head, top, keep, total, weights):
        values = [
            operands[value_at][start : start + count, lanes_of(head)]
            for _, _, value_at, start, count, _ in pieces
        ]
        values = values[0] if len(values) == 1 else jnp.concatenate(values, axis=0)
        mixed = lax.dot_general(
            values, weights, (((0,), (0,)), ((), ())), preferred_element_type=jnp.float32
        )
        if not first:
            mixed = mixed + keep * old_mixed_ref[lanes_of(head), :]
            total = total + keep * old_stats_ref[8 + head : 9 + head, :]
        if last:
            rest[0][:, lanes_of(head)] = (mixed / total).T
        else:
            rest[0][lanes_of(head), :] = mixed
            rest[1][head : head + 1, :] = top
            rest[1][8 + head : 9 + head, :] = total

    scores = score(0)
    waiting = None
    for head in range(heads):
        following = score(head + 1) if head + 1 < heads else None
        weighed = weigh(head, scores)
        if waiting is not None:
            mix(*waiting)
        waiting = (head, *weighed)
        scores = following
    mix(*waiting)


def attend(query, operands, pieces, valid, state=None, last=False):
    rows, width = query.shape
    heads = width // HD
    keys = sum(piece[4] for piece in pieces)
    first = state is None
    mixed = jax.ShapeDtypeStruct((width, rows), jnp.float32)
    stats = jax.ShapeDtypeStruct((16, rows), jnp.float32)
    out = jax.ShapeDtypeStruct((rows, width), jnp.float32)
    inputs = [valid, query, *operands] + ([] if first else list(state))
    vmem = pl.BlockSpec(memory_space=pltpu.VMEM)
    aliases = {}
    if not first and not last:
        aliases = {len(inputs) - 2: 0, len(inputs) - 1: 1}
    moved = 2 * (query.size + sum(operand.size for operand in operands)) + 8 * rows * width
    return pl.pallas_call(
        functools.partial(attend_kernel, pieces, first, last, len(operands)),
        out_shape=out if last else (mixed, stats),
        in_specs=[pl.BlockSpec(memory_space=pltpu.SMEM)] + [vmem] * (len(inputs) - 1),
        out_specs=vmem if last else (vmem, vmem),
        input_output_aliases=aliases,
        compiler_params=pltpu.CompilerParams(vmem_limit_bytes=VMEM_LIMIT),
        cost_estimate=pl.CostEstimate(
            flops=4 * rows * keys * width,
            bytes_accessed=moved,
            transcendentals=rows * keys * heads,
        ),
    )(*inputs)


def on_device(query_proj, key_proj, value_proj, query_gain, key_gain, key_blocks):
    rows, width = query_proj.shape
    width_total = width * lax.axis_size("heads")
    frame_count = lax.axis_size("frames")
    frame = lax.axis_index("frames")
    half, quarter = rows // 2, rows // 4
    smem = pl.BlockSpec(memory_space=pltpu.SMEM)
    vmem = pl.BlockSpec(memory_space=pltpu.VMEM)
    params = pltpu.CompilerParams(vmem_limit_bytes=VMEM_LIMIT)
    block = jax.ShapeDtypeStruct((rows, width), jnp.bfloat16)

    anywhere = pl.BlockSpec(memory_space=pltpu.HBM)
    devices = lax.axis_size("heads")
    own_value, squares = pl.pallas_call(
        gather_kernel,
        out_shape=(block, jax.ShapeDtypeStruct((devices, 2, rows), jnp.float32)),
        in_specs=[smem, anywhere, anywhere, anywhere],
        out_specs=(vmem, vmem),
        scratch_shapes=[pltpu.VMEM((rows, width), jnp.bfloat16)] * 3 + [pltpu.SemaphoreType.DMA((3,))],
        compiler_params=params,
        cost_estimate=pl.CostEstimate(flops=4 * rows * width, bytes_accessed=8 * rows * width, transcendentals=0),
    )(key_blocks, *(pltpu.with_memory_space_constraint(x, pltpu.HBM) for x in (query_proj, key_proj, value_proj)))
    near_value = [shift(own_value, step) for step in (1, -1)]
    squares = lax.all_to_all(squares, "heads", 0, 0)
    part = lambda count: jax.ShapeDtypeStruct((count, width), jnp.bfloat16)
    query, own_key, own_half, own_quarter = pl.pallas_call(
        functools.partial(norm_kernel, width_total),
        out_shape=(block, block, block, part(half)),
        in_specs=[smem] + [vmem] * 4 + [anywhere] * 2,
        out_specs=(vmem,) * 4,
        scratch_shapes=[pltpu.VMEM((rows, width), jnp.bfloat16)] * 2 + [pltpu.SemaphoreType.DMA((2,))],
        compiler_params=params,
        cost_estimate=pl.CostEstimate(flops=6 * rows * width, bytes_accessed=12 * rows * width, transcendentals=0),
    )(
        key_blocks,
        squares,
        query_gain.reshape(1, width),
        key_gain.reshape(1, width),
        own_value,
        query_proj,
        key_proj,
    )
    distance = jnp.arange(1, 8, dtype=jnp.int32)
    valid = jnp.concatenate([frame - distance >= 0, frame + distance < frame_count]).astype(jnp.int32)

    def flag(side, steps):
        return side * 7 + steps - 1

    both = (1, -1)
    sides = (0, 1)
    near_key = [shift(own_key, step) for step in both]
    state = attend(query, [own_key, own_value], [(0, 0, 1, 0, rows, None)], valid)
    own_half, own_quarter, near_value, state = lax.optimization_barrier(
        (own_half, own_quarter, near_value, state)
    )
    third = [shift(own_half, 3 * step) for step in both]
    fourth = [shift(own_quarter, 4 * step) for step in both]
    *near_key, state = lax.optimization_barrier((*near_key, state))
    relayed = [pack([near_key[side], near_value[side]], [(0, 0, half), (1, 0, half)]) for side in sides]
    second = [shift(value, step) for value, step in zip(relayed, both)]
    passed = [
        pack(
            [near_key[side], near_value[side], third[side]],
            [(0, 0, quarter), (2, 0, quarter), (1, 0, quarter), (2, half, quarter)],
        )
        for side in sides
    ]
    far = [shift(value, 4 * step) for value, step in zip(passed, both)]
    near_key = list(lax.optimization_barrier((*near_key, *relayed, *passed))[:2])
    state = attend(
        query,
        [*near_key, *near_value],
        [(side, 0, 2 + side, 0, rows, flag(side, 1)) for side in sides],
        valid,
        state,
    )
    state = attend(
        query,
        [*third, *fourth],
        [(side, 0, side, half, half, flag(side, 3)) for side in sides]
        + [(2 + side, 0, 2 + side, quarter, quarter, flag(side, 4)) for side in sides],
        valid,
        state,
    )
    *second, state = lax.optimization_barrier((*second, state))
    sixth = [
        shift(pack([second[side]], [(0, 0, quarter), (0, half, quarter)]), 4 * step)
        for side, step in enumerate(both)
    ]
    state = attend(
        query,
        second,
        [(side, 0, side, half, half, flag(side, 2)) for side in sides],
        valid,
        state,
    )
    state = attend(
        query,
        far,
        [
            (side, place * quarter, side, (2 + place) * quarter, quarter, flag(side, steps))
            for side in sides
            for place, steps in enumerate((5, 7))
        ],
        valid,
        state,
    )
    return attend(
        query,
        sixth,
        [(side, 0, side, quarter, quarter, flag(side, 6)) for side in sides],
        valid,
        state,
        last=True,
    )


def solution(mesh):
    placed = (
        P("frames", "heads"),
        P("frames", "heads"),
        P("frames", "heads"),
        P("heads"),
        P("heads"),
        P("frames", None),
    )
    return jax.shard_map(
        on_device, mesh=mesh, in_specs=placed, out_specs=P("frames", "heads"), check_vma=False
    )
```

time: 126 us -> 112 us (0.89)
  the two profiles are of different devices: /device:TPU:414 before, /device:TPU:224 now
where the time goes in v2:
time: 112 us
  starting transfers between devices  57.5 us (51%)
  Pallas kernels  26.9 us (24%)
  waiting for transfers between devices  26.3 us (23%)
    ppermute x14, starting transfers between devices, shift(): lax.ppermute(value, 'frames', [(source, source + steps) for source in ran...  53.2 us
    ppermute x14, waiting for transfers between devices, shift(): lax.ppermute(value, 'frames', [(source, source + steps) for source in ran...  20.9 us
    pallas_call x6, Pallas kernels, attend(): pl.pallas_call(functools.partial(attend_kernel, pieces, first, last, len(...  19.2 us
    all_to_all x1, waiting for transfers between devices, on_device(): squares = lax.all_to_all(squares, 'heads', 0, 0)  5.41 us
    all_to_all x1, starting transfers between devices, on_device(): squares = lax.all_to_all(squares, 'heads', 0, 0)  4.31 us
    pallas_call x6, Pallas kernels, pack(): pl.pallas_call(functools.partial(pack_kernel, parts), out_shape=jax.Shape...  3.11 us
    pallas_call x1, Pallas kernels, on_device(): pl.pallas_call(gather_kernel, out_shape=(block, jax.ShapeDtypeStruct((dev...  2.86 us
  transfers between devices with their start and end apart: 15, of which 5 were waited for; matrix products, arithmetic and copies ran while one was open for 0% of the time, Pallas kernels for 19%

profile of v2, /device:TPU:224, one launch (start us, length us, event | category | flops | bytes accessed | tf_op | source)
XLA Modules:
  0.0 111.9 jit_solution(13138098059229982275)
XLA Ops:
  0.0 0.0 copy-start
  0.0 0.0 copy-start.1
  0.0 0.0 copy-start.2
  0.0 0.8 copy-done.2
  0.8 0.0 copy-start.4
  0.8 0.0 copy-start.5
  0.8 0.0 copy-start.3
  0.8 2.9 %shard_map.64 = (bf16[512,640]{1,0:T(8,128)(2,1)S(1)}, f32[8,2,512]{2,1,0:T(2,128)}) custom-call(s32[1,16]{1,0:T(1,128)S(1)} %copy-done.2, bf16[512,640]{1,0:T(8,128)(2,1)} %query_hbm.3, bf16[512,640]{1,0:T(8,128)(2,1)} %key_hbm.3, bf16[512,640]{1,0:T(8,128)(2,1)} %value_hbm.1), custom_call_target="tpu_custom_call" | custom-call | flops 1310720 | bytes 2621440 | tf_op jit(solution)/shard_map/pallas_call | solution.py:273
  3.6 3.5 %collective-permute-start.2 = (bf16[512,640]{1,0:T(8,128)(2,1)S(1)}, bf16[512,640]{1,0:T(8,128)(2,1)S(1)}, u32[]{:S(2)}, u32[]{:S(2)}) collective-permute-start(bf16[512,640]{1,0:T(8,128)(2,1)S(1)} %get-tuple-element.38.ranked_value_ref.refs_1_), channel_id=1, source_target_pairs={{0,1},{1,2},{2,3},{3,4},{4,5},{5,6},{6,7},{7,8},{8,9},{9,10},{10,1... | collective-permute-start | bytes 1966088 | tf_op jit(solution)/shard_map/ppermute | solution.py:21
  7.1 4.5 %collective-permute-start.3 = (bf16[512,640]{1,0:T(8,128)(2,1)S(1)}, bf16[512,640]{1,0:T(8,128)(2,1)S(1)}, u32[]{:S(2)}, u32[]{:S(2)}) collective-permute-start(bf16[512,640]{1,0:T(8,128)(2,1)S(1)} %get-tuple-element.38.ranked_value_ref.refs_1_), channel_id=1, source_target_pairs={{1,0},{2,1},{3,2},{4,3},{5,4},{6,5},{7,6},{8,7},{9,8},{10,9},{11,1... | collective-permute-start | bytes 1966088 | tf_op jit(solution)/shard_map/ppermute | solution.py:21
  11.6 4.3 %all-to-all-start = ((f32[8,2,512]{2,1,0:T(2,128)}), f32[8,2,512]{2,1,0:T(2,128)S(1)}, u32[]{:S(2)}, u32[]{:S(2)}) async-start(f32[8,2,512]{2,1,0:T(2,128)} %get-tuple-element.37), calls=%async_computation | async-start | bytes 65536 | tf_op jit(solution)/shard_map/all_to_all | solution.py:283
  15.9 0.0 copy-done.4
  15.9 0.0 copy-done.5
  16.0 5.4 %all-to-all-done.squares_ref = f32[8,2,512]{2,1,0:T(2,128)S(1)} async-done(((f32[8,2,512]{2,1,0:T(2,128)}), f32[8,2,512]{2,1,0:T(2,128)S(1)}, u32[]{:S(2)}, u32[]{:S(2)}) %all-to-all-start) | async-done | bytes 32800 | tf_op jit(solution)/shard_map/all_to_all | solution.py:283
  21.4 0.0 copy-done
  21.4 0.0 copy-done.1
  21.4 0.0 copy-done.3
  21.4 1.7 %shard_map.65 = (bf16[512,640]{1,0:T(8,128)(2,1)S(1)}, bf16[512,640]{1,0:T(8,128)(2,1)S(1)}, bf16[512,640]{1,0:T(8,128)(2,1)S(1)}, bf16[256,640]{1,0:T(8,128)(2,1)S(1)}) custom-call(s32[1,16]{1,0:T(1,128)S(1)} %copy-done.3, f32[8,2,512]{2,1,0:T(2,128)S(1)} %all-to-all-done.squares_ref, f32[1,640]{1,0:T(1,128)S(1)} %reshape.6.query_gain_ref, ...), custom_call_target="tpu_custom_call" | custom-call | flops 1966080 | bytes 3932160 | tf_op jit(solution)/shard_map/pallas_call | solution.py:285
  23.1 1.9 %collective-permute-start = (bf16[512,640]{1,0:T(8,128)(2,1)S(1)}, bf16[512,640]{1,0:T(8,128)(2,1)S(1)}, u32[]{:S(2)}, u32[]{:S(2)}) collective-permute-start(bf16[512,640]{1,0:T(8,128)(2,1)S(1)} %get-tuple-element.40.refs_0_), channel_id=1, source_target_pairs={{0,1},{1,2},{2,3},{3,4},{4,5},{5,6},{6,7},{7,8},{8,9},{9,10},{10,1... | collective-permute-start | bytes 1966088 | tf_op jit(solution)/shard_map/ppermute | solution.py:21
  25.0 6.0 %collective-permute-start.1 = (bf16[512,640]{1,0:T(8,128)(2,1)S(1)}, bf16[512,640]{1,0:T(8,128)(2,1)S(1)}, u32[]{:S(2)}, u32[]{:S(2)}) collective-permute-start(bf16[512,640]{1,0:T(8,128)(2,1)S(1)} %get-tuple-element.40.refs_0_), channel_id=1, source_target_pairs={{1,0},{2,1},{3,2},{4,3},{5,4},{6,5},{7,6},{8,7},{9,8},{10,9},{11,1... | collective-permute-start | bytes 1966088 | tf_op jit(solution)/shard_map/ppermute | solution.py:21
  31.1 0.1 add_convert_fusion.valid_ref
  31.2 2.5 %shard_map.66 = (f32[640,512]{1,0:T(8,128)S(1)}, f32[16,512]{1,0:T(8,128)S(1)}) custom-call(s32[14]{0:T(128)S(1)} %add_convert_fusion.valid_ref, bf16[512,640]{1,0:T(8,128)(2,1)S(1)} %get-tuple-element.39.query_ref, bf16[512,640]{1,0:T(8,128)(2,1)S(1)} %get-tuple-element.40.refs_0_, bf16[512,640]{1,0:T(8,128)(2,1)S(1)} %get-tuple-element.38.ranked_value_ref.refs_1_), custom_call_target="tpu_custom_call" | custom-call | flops 671088640 | bytes 4587520 | tf_op jit(solution)/shard_map/pallas_call | solution.py:245
  33.7 0.0 collective-permute-done.2.refs_1_.refs_2_
  33.7 0.0 collective-permute-done.3.refs_1_.refs_3_
  33.7 1.9 %collective-permute-start.7 = (bf16[512,640]{1,0:T(8,128)(2,1)S(1)}, bf16[512,640]{1,0:T(8,128)(2,1)S(1)}, u32[]{:S(2)}, u32[]{:S(2)}) collective-permute-start(bf16[512,640]{1,0:T(8,128)(2,1)S(1)} %get-tuple-element.51), channel_id=1, source_target_pairs={{3,0},{4,1},{5,2},{6,3},{7,4},{8,5},{9,6},{10,7},{11,8},{12,9},{13... | collective-permute-start | bytes 1966088 | tf_op jit(solution)/shard_map/ppermute | solution.py:21
  35.7 5.1 %collective-permute-start.6 = (bf16[512,640]{1,0:T(8,128)(2,1)S(1)}, bf16[512,640]{1,0:T(8,128)(2,1)S(1)}, u32[]{:S(2)}, u32[]{:S(2)}) collective-permute-start(bf16[512,640]{1,0:T(8,128)(2,1)S(1)} %get-tuple-element.51), channel_id=1, source_target_pairs={{0,3},{1,4},{2,5},{3,6},{4,7},{5,8},{6,9},{7,10},{8,11},{9,12},{10... | collective-permute-start | bytes 1966088 | tf_op jit(solution)/shard_map/ppermute | solution.py:21
  40.8 7.5 %collective-permute-start.8 = (bf16[256,640]{1,0:T(8,128)(2,1)S(1)}, bf16[256,640]{1,0:T(8,128)(2,1)S(1)}, u32[]{:S(2)}, u32[]{:S(2)}) collective-permute-start(bf16[256,640]{1,0:T(8,128)(2,1)S(1)} %get-tuple-element.52), channel_id=1, source_target_pairs={{0,4},{1,5},{2,6},{3,7},{4,8},{5,9},{6,10},{7,11},{8,12},{9,13},{1... | collective-permute-start | bytes 983048 | tf_op jit(solution)/shard_map/ppermute | solution.py:21
  48.3 0.0 collective-permute-done.refs_0_
  48.3 9.4 %collective-permute-done.1.refs_0_.refs_1_ = bf16[512,640]{1,0:T(8,128)(2,1)S(1)} collective-permute-done((bf16[512,640]{1,0:T(8,128)(2,1)S(1)}, bf16[512,640]{1,0:T(8,128)(2,1)S(1)}, u32[]{:S(2)}, u32[]{:S(2)}) %collective-permute-start.1) | collective-permute-done | bytes 655392 | tf_op jit(solution)/shard_map/ppermute | solution.py:21
  57.7 0.2 shard_map.68
  57.9 3.6 %collective-permute-start.5 = (bf16[512,640]{1,0:T(8,128)(2,1)S(1)}, bf16[512,640]{1,0:T(8,128)(2,1)S(1)}, u32[]{:S(2)}, u32[]{:S(2)}) collective-permute-start(bf16[512,640]{1,0:T(8,128)(2,1)S(1)} %shard_map.68), channel_id=1, source_target_pairs={{1,0},{2,1},{3,2},{4,3},{5,4},{6,5},{7,6},{8,7},{9,8},{10,9},{11,1... | collective-permute-start | bytes 1966088 | tf_op jit(solution)/shard_map/ppermute | solution.py:21
  61.5 0.2 shard_map.67
  61.7 2.3 %collective-permute-start.4 = (bf16[512,640]{1,0:T(8,128)(2,1)S(1)}, bf16[512,640]{1,0:T(8,128)(2,1)S(1)}, u32[]{:S(2)}, u32[]{:S(2)}) collective-permute-start(bf16[512,640]{1,0:T(8,128)(2,1)S(1)} %shard_map.67), channel_id=1, source_target_pairs={{0,1},{1,2},{2,3},{3,4},{4,5},{5,6},{6,7},{7,8},{8,9},{9,10},{10,1... | collective-permute-start | bytes 1966088 | tf_op jit(solution)/shard_map/ppermute | solution.py:21
  64.0 0.0 collective-permute-done.7.refs_2_.refs_1_
  64.0 2.0 %collective-permute-start.9 = (bf16[256,640]{1,0:T(8,128)(2,1)S(1)}, bf16[256,640]{1,0:T(8,128)(2,1)S(1)}, u32[]{:S(2)}, u32[]{:S(2)}) collective-permute-start(bf16[256,640]{1,0:T(8,128)(2,1)S(1)} %get-tuple-element.52), channel_id=1, source_target_pairs={{4,0},{5,1},{6,2},{7,3},{8,4},{9,5},{10,6},{11,7},{12,8},{13,9},{1... | collective-permute-start | bytes 983048 | tf_op jit(solution)/shard_map/ppermute | solution.py:21
  66.0 0.9 shard_map.70
  66.9 0.0 collective-permute-done.6.refs_2_.refs_0_
  66.9 2.0 %collective-permute-start.13 = (bf16[512,640]{1,0:T(8,128)(2,1)S(1)}, bf16[512,640]{1,0:T(8,128)(2,1)S(1)}, u32[]{:S(2)}, u32[]{:S(2)}) collective-permute-start(bf16[512,640]{1,0:T(8,128)(2,1)S(1)} %shard_map.70), channel_id=1, source_target_pairs={{4,0},{5,1},{6,2},{7,3},{8,4},{9,5},{10,6},{11,7},{12,8},{13,9},{1... | collective-permute-start | bytes 1966088 | tf_op jit(solution)/shard_map/ppermute | solution.py:21
  69.0 0.9 shard_map.69
  69.9 0.0 collective-permute-done.8.refs_2_
  69.9 6.9 %collective-permute-start.12 = (bf16[512,640]{1,0:T(8,128)(2,1)S(1)}, bf16[512,640]{1,0:T(8,128)(2,1)S(1)}, u32[]{:S(2)}, u32[]{:S(2)}) collective-permute-start(bf16[512,640]{1,0:T(8,128)(2,1)S(1)} %shard_map.69), channel_id=1, source_target_pairs={{0,4},{1,5},{2,6},{3,7},{4,8},{5,9},{6,10},{7,11},{8,12},{9,13},{1... | collective-permute-start | bytes 1966088 | tf_op jit(solution)/shard_map/ppermute | solution.py:21
  76.8 4.4 %shard_map.71 = (f32[640,512]{1,0:T(8,128)S(1)}, f32[16,512]{1,0:T(8,128)S(1)}) custom-call(s32[14]{0:T(128)S(1)} %add_convert_fusion.valid_ref, bf16[512,640]{1,0:T(8,128)(2,1)S(1)} %get-tuple-element.39.query_ref, bf16[512,640]{1,0:T(8,128)(2,1)S(1)} %collective-permute-done.refs_0_, ...), custom_call_target="tpu_custom_call", output_to_operand_aliasing={{0}: (6, {}), {1}: (7, {})} | custom-call | flops 1342177280 | bytes 5898240 | tf_op jit(solution)/shard_map/pallas_call | solution.py:245
  81.2 8.5 %collective-permute-done.9.refs_3_ = bf16[256,640]{1,0:T(8,128)(2,1)S(1)} collective-permute-done((bf16[256,640]{1,0:T(8,128)(2,1)S(1)}, bf16[256,640]{1,0:T(8,128)(2,1)S(1)}, u32[]{:S(2)}, u32[]{:S(2)}) %collective-permute-start.9) | collective-permute-done | bytes 327712 | tf_op jit(solution)/shard_map/ppermute | solution.py:21
  89.7 3.7 %shard_map.72 = (f32[640,512]{1,0:T(8,128)S(1)}, f32[16,512]{1,0:T(8,128)S(1)}) custom-call(s32[14]{0:T(128)S(1)} %add_convert_fusion.valid_ref, bf16[512,640]{1,0:T(8,128)(2,1)S(1)} %get-tuple-element.39.query_ref, bf16[512,640]{1,0:T(8,128)(2,1)S(1)} %collective-permute-done.6.refs_2_.refs_0_, ...), custom_call_target="tpu_custom_call", output_to_operand_aliasing={{0}: (6, {}), {1}: (7, {})} | custom-call | flops 1006632960 | bytes 5242880 | tf_op jit(solution)/shard_map/pallas_call | solution.py:245
  93.4 0.0 collective-permute-done.5.refs_0_.refs_1_
  93.4 0.0 collective-permute-done.4.refs_0_
  93.4 0.4 shard_map.73
  93.9 1.9 %collective-permute-start.10 = (bf16[256,640]{1,0:T(8,128)(2,1)S(1)}, bf16[256,640]{1,0:T(8,128)(2,1)S(1)}, u32[]{:S(2)}, u32[]{:S(2)}) collective-permute-start(bf16[256,640]{1,0:T(8,128)(2,1)S(1)} %shard_map.73), channel_id=1, source_target_pairs={{0,4},{1,5},{2,6},{3,7},{4,8},{5,9},{6,10},{7,11},{8,12},{9,13},{1... | collective-permute-start | bytes 983048 | tf_op jit(solution)/shard_map/ppermute | solution.py:21
  95.8 0.4 shard_map.74
  96.3 4.1 %collective-permute-start.11 = (bf16[256,640]{1,0:T(8,128)(2,1)S(1)}, bf16[256,640]{1,0:T(8,128)(2,1)S(1)}, u32[]{:S(2)}, u32[]{:S(2)}) collective-permute-start(bf16[256,640]{1,0:T(8,128)(2,1)S(1)} %shard_map.74), channel_id=1, source_target_pairs={{4,0},{5,1},{6,2},{7,3},{8,4},{9,5},{10,6},{11,7},{12,8},{13,9},{1... | collective-permute-start | bytes 983048 | tf_op jit(solution)/shard_map/ppermute | solution.py:21
  100.4 2.8 %shard_map.75 = (f32[640,512]{1,0:T(8,128)S(1)}, f32[16,512]{1,0:T(8,128)S(1)}) custom-call(s32[14]{0:T(128)S(1)} %add_convert_fusion.valid_ref, bf16[512,640]{1,0:T(8,128)(2,1)S(1)} %get-tuple-element.39.query_ref, bf16[512,640]{1,0:T(8,128)(2,1)S(1)} %collective-permute-done.4.refs_0_, ...), custom_call_target="tpu_custom_call", output_to_operand_aliasing={{0}: (4, {}), {1}: (5, {})} | custom-call | flops 671088640 | bytes 4587520 | tf_op jit(solution)/shard_map/pallas_call | solution.py:245
  103.2 0.5 collective-permute-done.13.refs_1_
  103.7 0.0 collective-permute-done.12.refs_0_
  103.7 2.8 %shard_map.76 = (f32[640,512]{1,0:T(8,128)S(1)}, f32[16,512]{1,0:T(8,128)S(1)}) custom-call(s32[14]{0:T(128)S(1)} %add_convert_fusion.valid_ref, bf16[512,640]{1,0:T(8,128)(2,1)S(1)} %get-tuple-element.39.query_ref, bf16[512,640]{1,0:T(8,128)(2,1)S(1)} %collective-permute-done.12.refs_0_, ...), custom_call_target="tpu_custom_call", output_to_operand_aliasing={{0}: (4, {}), {1}: (5, {})} | custom-call | flops 671088640 | bytes 4587520 | tf_op jit(solution)/shard_map/pallas_call | solution.py:245
  106.5 0.0 collective-permute-done.10.refs_0_
  106.5 2.4 %collective-permute-done.11.refs_1_ = bf16[256,640]{1,0:T(8,128)(2,1)S(1)} collective-permute-done((bf16[256,640]{1,0:T(8,128)(2,1)S(1)}, bf16[256,640]{1,0:T(8,128)(2,1)S(1)}, u32[]{:S(2)}, u32[]{:S(2)}) %collective-permute-start.11) | collective-permute-done | bytes 327712 | tf_op jit(solution)/shard_map/ppermute | solution.py:21
  108.9 3.0 %shard_map.77 = f32[512,640]{1,0:T(8,128)} custom-call(s32[14]{0:T(128)S(1)} %add_convert_fusion.valid_ref, bf16[512,640]{1,0:T(8,128)(2,1)S(1)} %get-tuple-element.39.query_ref, bf16[256,640]{1,0:T(8,128)(2,1)S(1)} %collective-permute-done.10.refs_0_, bf16[256,640]{1,0:T(8,128)(2,1)S(1)} %collective-permute-done.11.refs_1_, ...), custom_call_target="tpu_custom_call" | custom-call | flops 335544320 | bytes 3932160 | tf_op jit(solution)/shard_map/pallas_call | solution.py:245
  (3 shorter events, 0.0 us)
Async XLA Ops:
  0.0 21.4 %copy-start = (bf16[512,640]{1,0:T(8,128)(2,1)S(1)}, bf16[512,640]{1,0:T(8,128)(2,1)}, u32[]{:S(2)}) copy-start(bf16[512,640]{1,0:T(8,128)(2,1)} %query_hbm.3) | copy-start | bytes 1966084
  0.0 21.4 %copy-start.1 = (bf16[512,640]{1,0:T(8,128)(2,1)S(1)}, bf16[512,640]{1,0:T(8,128)(2,1)}, u32[]{:S(2)}) copy-start(bf16[512,640]{1,0:T(8,128)(2,1)} %key_hbm.3) | copy-start | bytes 1966084
  0.0 0.8 copy-start.2
  0.8 15.2 %copy-start.4 = (f32[640]{0:T(1024)S(1)}, f32[640]{0:T(1024)}, u32[]{:S(2)}) copy-start(f32[640]{0:T(1024)} %param.9) | copy-start | bytes 7684
  0.8 15.2 %copy-start.5 = (f32[640]{0:T(1024)S(1)}, f32[640]{0:T(1024)}, u32[]{:S(2)}) copy-start(f32[640]{0:T(1024)} %param.10) | copy-start | bytes 7684
  0.8 20.6 %copy-start.3 = (s32[1,16]{1,0:T(1,128)S(1)}, s32[1,16]{1,0:T(1,128)}, u32[]{:S(2)}) copy-start(s32[1,16]{1,0:T(1,128)} %blocks_ref.3) | copy-start | bytes 196
  3.6 30.1 %collective-permute-start.2 = (bf16[512,640]{1,0:T(8,128)(2,1)S(1)}, bf16[512,640]{1,0:T(8,128)(2,1)S(1)}, u32[]{:S(2)}, u32[]{:S(2)}) collective-permute-start(bf16[512,640]{1,0:T(8,128)(2,1)S(1)} %get-tuple-element.38.ranked_value_ref.refs_1_), channel_id=1, source_target_pairs={{0,1},{1,2},{2,3},{3,4},{4,5},{5,6},{6,7},{7,8},{8,9},{9,10},{10,1... | collective-permute-start | bytes 1966088 | tf_op jit(solution)/shard_map/ppermute | solution.py:21
  7.1 26.6 %collective-permute-start.3 = (bf16[512,640]{1,0:T(8,128)(2,1)S(1)}, bf16[512,640]{1,0:T(8,128)(2,1)S(1)}, u32[]{:S(2)}, u32[]{:S(2)}) collective-permute-start(bf16[512,640]{1,0:T(8,128)(2,1)S(1)} %get-tuple-element.38.ranked_value_ref.refs_1_), channel_id=1, source_target_pairs={{1,0},{2,1},{3,2},{4,3},{5,4},{6,5},{7,6},{8,7},{9,8},{10,9},{11,1... | collective-permute-start | bytes 1966088 | tf_op jit(solution)/shard_map/ppermute | solution.py:21
  11.6 9.8 %all-to-all-start = ((f32[8,2,512]{2,1,0:T(2,128)}), f32[8,2,512]{2,1,0:T(2,128)S(1)}, u32[]{:S(2)}, u32[]{:S(2)}) async-start(f32[8,2,512]{2,1,0:T(2,128)} %get-tuple-element.37), calls=%async_computation | async-start | bytes 65536 | tf_op jit(solution)/shard_map/all_to_all | solution.py:283
  23.1 25.2 %collective-permute-start = (bf16[512,640]{1,0:T(8,128)(2,1)S(1)}, bf16[512,640]{1,0:T(8,128)(2,1)S(1)}, u32[]{:S(2)}, u32[]{:S(2)}) collective-permute-start(bf16[512,640]{1,0:T(8,128)(2,1)S(1)} %get-tuple-element.40.refs_0_), channel_id=1, source_target_pairs={{0,1},{1,2},{2,3},{3,4},{4,5},{5,6},{6,7},{7,8},{8,9},{9,10},{10,1... | collective-permute-start | bytes 1966088 | tf_op jit(solution)/shard_map/ppermute | solution.py:21
  25.0 32.6 %collective-permute-start.1 = (bf16[512,640]{1,0:T(8,128)(2,1)S(1)}, bf16[512,640]{1,0:T(8,128)(2,1)S(1)}, u32[]{:S(2)}, u32[]{:S(2)}) collective-permute-start(bf16[512,640]{1,0:T(8,128)(2,1)S(1)} %get-tuple-element.40.refs_0_), channel_id=1, source_target_pairs={{1,0},{2,1},{3,2},{4,3},{5,4},{6,5},{7,6},{8,7},{9,8},{10,9},{11,1... | collective-permute-start | bytes 1966088 | tf_op jit(solution)/shard_map/ppermute | solution.py:21
  33.7 30.3 %collective-permute-start.7 = (bf16[512,640]{1,0:T(8,128)(2,1)S(1)}, bf16[512,640]{1,0:T(8,128)(2,1)S(1)}, u32[]{:S(2)}, u32[]{:S(2)}) collective-permute-start(bf16[512,640]{1,0:T(8,128)(2,1)S(1)} %get-tuple-element.51), channel_id=1, source_target_pairs={{3,0},{4,1},{5,2},{6,3},{7,4},{8,5},{9,6},{10,7},{11,8},{12,9},{13... | collective-permute-start | bytes 1966088 | tf_op jit(solution)/shard_map/ppermute | solution.py:21
  35.7 31.3 %collective-permute-start.6 = (bf16[512,640]{1,0:T(8,128)(2,1)S(1)}, bf16[512,640]{1,0:T(8,128)(2,1)S(1)}, u32[]{:S(2)}, u32[]{:S(2)}) collective-permute-start(bf16[512,640]{1,0:T(8,128)(2,1)S(1)} %get-tuple-element.51), channel_id=1, source_target_pairs={{0,3},{1,4},{2,5},{3,6},{4,7},{5,8},{6,9},{7,10},{8,11},{9,12},{10... | collective-permute-start | bytes 1966088 | tf_op jit(solution)/shard_map/ppermute | solution.py:21
  40.8 29.1 %collective-permute-start.8 = (bf16[256,640]{1,0:T(8,128)(2,1)S(1)}, bf16[256,640]{1,0:T(8,128)(2,1)S(1)}, u32[]{:S(2)}, u32[]{:S(2)}) collective-permute-start(bf16[256,640]{1,0:T(8,128)(2,1)S(1)} %get-tuple-element.52), channel_id=1, source_target_pairs={{0,4},{1,5},{2,6},{3,7},{4,8},{5,9},{6,10},{7,11},{8,12},{9,13},{1... | collective-permute-start | bytes 983048 | tf_op jit(solution)/shard_map/ppermute | solution.py:21
  57.9 35.5 %collective-permute-start.5 = (bf16[512,640]{1,0:T(8,128)(2,1)S(1)}, bf16[512,640]{1,0:T(8,128)(2,1)S(1)}, u32[]{:S(2)}, u32[]{:S(2)}) collective-permute-start(bf16[512,640]{1,0:T(8,128)(2,1)S(1)} %shard_map.68), channel_id=1, source_target_pairs={{1,0},{2,1},{3,2},{4,3},{5,4},{6,5},{7,6},{8,7},{9,8},{10,9},{11,1... | collective-permute-start | bytes 1966088 | tf_op jit(solution)/shard_map/ppermute | solution.py:21
  61.7 31.7 %collective-permute-start.4 = (bf16[512,640]{1,0:T(8,128)(2,1)S(1)}, bf16[512,640]{1,0:T(8,128)(2,1)S(1)}, u32[]{:S(2)}, u32[]{:S(2)}) collective-permute-start(bf16[512,640]{1,0:T(8,128)(2,1)S(1)} %shard_map.67), channel_id=1, source_target_pairs={{0,1},{1,2},{2,3},{3,4},{4,5},{5,6},{6,7},{7,8},{8,9},{9,10},{10,1... | collective-permute-start | bytes 1966088 | tf_op jit(solution)/shard_map/ppermute | solution.py:21
  64.0 25.7 %collective-permute-start.9 = (bf16[256,640]{1,0:T(8,128)(2,1)S(1)}, bf16[256,640]{1,0:T(8,128)(2,1)S(1)}, u32[]{:S(2)}, u32[]{:S(2)}) collective-permute-start(bf16[256,640]{1,0:T(8,128)(2,1)S(1)} %get-tuple-element.52), channel_id=1, source_target_pairs={{4,0},{5,1},{6,2},{7,3},{8,4},{9,5},{10,6},{11,7},{12,8},{13,9},{1... | collective-permute-start | bytes 983048 | tf_op jit(solution)/shard_map/ppermute | solution.py:21
  66.9 36.8 %collective-permute-start.13 = (bf16[512,640]{1,0:T(8,128)(2,1)S(1)}, bf16[512,640]{1,0:T(8,128)(2,1)S(1)}, u32[]{:S(2)}, u32[]{:S(2)}) collective-permute-start(bf16[512,640]{1,0:T(8,128)(2,1)S(1)} %shard_map.70), channel_id=1, source_target_pairs={{4,0},{5,1},{6,2},{7,3},{8,4},{9,5},{10,6},{11,7},{12,8},{13,9},{1... | collective-permute-start | bytes 1966088 | tf_op jit(solution)/shard_map/ppermute | solution.py:21
  69.9 33.8 %collective-permute-start.12 = (bf16[512,640]{1,0:T(8,128)(2,1)S(1)}, bf16[512,640]{1,0:T(8,128)(2,1)S(1)}, u32[]{:S(2)}, u32[]{:S(2)}) collective-permute-start(bf16[512,640]{1,0:T(8,128)(2,1)S(1)} %shard_map.69), channel_id=1, source_target_pairs={{0,4},{1,5},{2,6},{3,7},{4,8},{5,9},{6,10},{7,11},{8,12},{9,13},{1... | collective-permute-start | bytes 1966088 | tf_op jit(solution)/shard_map/ppermute | solution.py:21
  93.9 12.6 %collective-permute-start.10 = (bf16[256,640]{1,0:T(8,128)(2,1)S(1)}, bf16[256,640]{1,0:T(8,128)(2,1)S(1)}, u32[]{:S(2)}, u32[]{:S(2)}) collective-permute-start(bf16[256,640]{1,0:T(8,128)(2,1)S(1)} %shard_map.73), channel_id=1, source_target_pairs={{0,4},{1,5},{2,6},{3,7},{4,8},{5,9},{6,10},{7,11},{8,12},{9,13},{1... | collective-permute-start | bytes 983048 | tf_op jit(solution)/shard_map/ppermute | solution.py:21
  96.3 12.7 %collective-permute-start.11 = (bf16[256,640]{1,0:T(8,128)(2,1)S(1)}, bf16[256,640]{1,0:T(8,128)(2,1)S(1)}, u32[]{:S(2)}, u32[]{:S(2)}) collective-permute-start(bf16[256,640]{1,0:T(8,128)(2,1)S(1)} %shard_map.74), channel_id=1, source_target_pairs={{4,0},{5,1},{6,2},{7,3},{8,4},{9,5},{10,6},{11,7},{12,8},{13,9},{1... | collective-permute-start | bytes 983048 | tf_op jit(solution)/shard_map/ppermute | solution.py:21

commit v3 on v2

--- a/solution.py
+++ b/solution.py
@@ -33,16 +33,32 @@
 
 
 def gather_kernel(
-    blocks_ref, query_hbm, key_hbm, value_hbm, ranked_ref, squares_ref, query_ref, key_ref, value_ref, sems
+    blocks_hbm,
+    query_hbm,
+    key_hbm,
+    value_hbm,
+    ranked_ref,
+    squares_ref,
+    blocks_ref,
+    query_ref,
+    key_ref,
+    value_ref,
+    sems,
 ):
     copies = [
         pltpu.make_async_copy(source, target, sems.at[place])
         for place, (source, target) in enumerate(
-            ((value_hbm, value_ref), (query_hbm, query_ref), (key_hbm, key_ref))
+            (
+                (value_hbm, value_ref),
+                (query_hbm, query_ref),
+                (key_hbm, key_ref),
+                (blocks_hbm, blocks_ref),
+            )
         )
     ]
     for copy in copies:
         copy.start()
+    copies[3].wait()
     copies[0].wait()
     block_count = blocks_ref.shape[1]
     size = value_ref.shape[0] // block_count
@@ -273,12 +289,19 @@
     own_value, squares = pl.pallas_call(
         gather_kernel,
         out_shape=(block, jax.ShapeDtypeStruct((devices, 2, rows), jnp.float32)),
-        in_specs=[smem, anywhere, anywhere, anywhere],
+        in_specs=[anywhere] * 4,
         out_specs=(vmem, vmem),
-        scratch_shapes=[pltpu.VMEM((rows, width), jnp.bfloat16)] * 3 + [pltpu.SemaphoreType.DMA((3,))],
+        scratch_shapes=[pltpu.SMEM(key_blocks.shape, jnp.int32)]
+        + [pltpu.VMEM((rows, width), jnp.bfloat16)] * 3
+        + [pltpu.SemaphoreType.DMA((4,))],
         compiler_params=params,
         cost_estimate=pl.CostEstimate(flops=4 * rows * width, bytes_accessed=8 * rows * width, transcendentals=0),
-    )(key_blocks, *(pltpu.with_memory_space_constraint(x, pltpu.HBM) for x in (query_proj, key_proj, value_proj)))
+    )(
+        *(
+            pltpu.with_memory_space_constraint(value, pltpu.HBM)
+            for value in (key_blocks, query_proj, key_proj, value_proj)
+        )
+    )
     near_value = [shift(own_value, step) for step in (1, -1)]
     squares = lax.all_to_all(squares, "heads", 0, 0)
     part = lambda count: jax.ShapeDtypeStruct((count, width), jnp.bfloat16)

time: 112 us -> 111 us (level)
  no operation moved by 1% of the time
where the time goes in v3:
time: 111 us
  starting transfers between devices  57.5 us (52%)
  Pallas kernels  26.5 us (24%)
  waiting for transfers between devices  26.3 us (24%)
    ppermute x14, starting transfers between devices, shift(): lax.ppermute(value, 'frames', [(source, source + steps) for source in ran...  53.2 us
    ppermute x14, waiting for transfers between devices, shift(): lax.ppermute(value, 'frames', [(source, source + steps) for source in ran...  20.9 us
    pallas_call x6, Pallas kernels, attend(): pl.pallas_call(functools.partial(attend_kernel, pieces, first, last, len(...  19.2 us
    all_to_all x1, waiting for transfers between devices, on_device(): squares = lax.all_to_all(squares, 'heads', 0, 0)  5.41 us
    all_to_all x1, starting transfers between devices, on_device(): squares = lax.all_to_all(squares, 'heads', 0, 0)  4.31 us
    pallas_call x6, Pallas kernels, pack(): pl.pallas_call(functools.partial(pack_kernel, parts), out_shape=jax.Shape...  3.11 us
    pallas_call x1, Pallas kernels, on_device(): pl.pallas_call(gather_kernel, out_shape=(block, jax.ShapeDtypeStruct((dev...  2.44 us
  transfers between devices with their start and end apart: 15, of which 5 were waited for; matrix products, arithmetic and copies ran while one was open for 0% of the time, Pallas kernels for 19%

profile of v3, /device:TPU:224, one launch (start us, length us, event | category | flops | bytes accessed | tf_op | source)
XLA Modules:
  0.0 110.8 jit_solution(389439966361012465)
XLA Ops:
  0.0 0.0 copy-start.2
  0.0 0.0 copy-start
  0.0 0.0 copy-start.1
  0.0 0.0 copy-start.3
  0.0 0.0 copy-start.4
  0.0 2.4 %shard_map.64 = (bf16[512,640]{1,0:T(8,128)(2,1)S(1)}, f32[8,2,512]{2,1,0:T(2,128)}) custom-call(s32[1,16]{1,0:T(1,128)} %blocks_ref.1, bf16[512,640]{1,0:T(8,128)(2,1)} %query_hbm.3, bf16[512,640]{1,0:T(8,128)(2,1)} %key_hbm.3, bf16[512,640]{1,0:T(8,128)(2,1)} %value_hbm.1), custom_call_target="tpu_custom_call" | custom-call | flops 1310720 | bytes 2621440 | tf_op jit(solution)/shard_map/pallas_call | solution.py:289
  2.5 3.5 %collective-permute-start.2 = (bf16[512,640]{1,0:T(8,128)(2,1)S(1)}, bf16[512,640]{1,0:T(8,128)(2,1)S(1)}, u32[]{:S(2)}, u32[]{:S(2)}) collective-permute-start(bf16[512,640]{1,0:T(8,128)(2,1)S(1)} %get-tuple-element.38.ranked_value_ref.refs_1_), channel_id=1, source_target_pairs={{0,1},{1,2},{2,3},{3,4},{4,5},{5,6},{6,7},{7,8},{8,9},{9,10},{10,1... | collective-permute-start | bytes 1966088 | tf_op jit(solution)/shard_map/ppermute | solution.py:21
  6.0 4.5 %collective-permute-start.3 = (bf16[512,640]{1,0:T(8,128)(2,1)S(1)}, bf16[512,640]{1,0:T(8,128)(2,1)S(1)}, u32[]{:S(2)}, u32[]{:S(2)}) collective-permute-start(bf16[512,640]{1,0:T(8,128)(2,1)S(1)} %get-tuple-element.38.ranked_value_ref.refs_1_), channel_id=1, source_target_pairs={{1,0},{2,1},{3,2},{4,3},{5,4},{6,5},{7,6},{8,7},{9,8},{10,9},{11,1... | collective-permute-start | bytes 1966088 | tf_op jit(solution)/shard_map/ppermute | solution.py:21
  10.4 4.3 %all-to-all-start = ((f32[8,2,512]{2,1,0:T(2,128)}), f32[8,2,512]{2,1,0:T(2,128)S(1)}, u32[]{:S(2)}, u32[]{:S(2)}) async-start(f32[8,2,512]{2,1,0:T(2,128)} %get-tuple-element.37), calls=%async_computation | async-start | bytes 65536 | tf_op jit(solution)/shard_map/all_to_all | solution.py:306
  14.8 0.0 copy-done.3
  14.8 0.0 copy-done.4
  14.8 5.4 %all-to-all-done.squares_ref = f32[8,2,512]{2,1,0:T(2,128)S(1)} async-done(((f32[8,2,512]{2,1,0:T(2,128)}), f32[8,2,512]{2,1,0:T(2,128)S(1)}, u32[]{:S(2)}, u32[]{:S(2)}) %all-to-all-start) | async-done | bytes 32800 | tf_op jit(solution)/shard_map/all_to_all | solution.py:306
  20.2 0.0 copy-done.2
  20.2 0.0 copy-done
  20.2 0.0 copy-done.1
  20.2 1.7 %shard_map.65 = (bf16[512,640]{1,0:T(8,128)(2,1)S(1)}, bf16[512,640]{1,0:T(8,128)(2,1)S(1)}, bf16[512,640]{1,0:T(8,128)(2,1)S(1)}, bf16[256,640]{1,0:T(8,128)(2,1)S(1)}) custom-call(s32[1,16]{1,0:T(1,128)S(1)} %copy-done.2, f32[8,2,512]{2,1,0:T(2,128)S(1)} %all-to-all-done.squares_ref, f32[1,640]{1,0:T(1,128)S(1)} %reshape.6.query_gain_ref, ...), custom_call_target="tpu_custom_call" | custom-call | flops 1966080 | bytes 3932160 | tf_op jit(solution)/shard_map/pallas_call | solution.py:308
  21.9 1.9 %collective-permute-start = (bf16[512,640]{1,0:T(8,128)(2,1)S(1)}, bf16[512,640]{1,0:T(8,128)(2,1)S(1)}, u32[]{:S(2)}, u32[]{:S(2)}) collective-permute-start(bf16[512,640]{1,0:T(8,128)(2,1)S(1)} %get-tuple-element.40.refs_0_), channel_id=1, source_target_pairs={{0,1},{1,2},{2,3},{3,4},{4,5},{5,6},{6,7},{7,8},{8,9},{9,10},{10,1... | collective-permute-start | bytes 1966088 | tf_op jit(solution)/shard_map/ppermute | solution.py:21
  23.9 6.0 %collective-permute-start.1 = (bf16[512,640]{1,0:T(8,128)(2,1)S(1)}, bf16[512,640]{1,0:T(8,128)(2,1)S(1)}, u32[]{:S(2)}, u32[]{:S(2)}) collective-permute-start(bf16[512,640]{1,0:T(8,128)(2,1)S(1)} %get-tuple-element.40.refs_0_), channel_id=1, source_target_pairs={{1,0},{2,1},{3,2},{4,3},{5,4},{6,5},{7,6},{8,7},{9,8},{10,9},{11,1... | collective-permute-start | bytes 1966088 | tf_op jit(solution)/shard_map/ppermute | solution.py:21
  29.9 0.1 add_convert_fusion.valid_ref
  30.0 2.5 %shard_map.66 = (f32[640,512]{1,0:T(8,128)S(1)}, f32[16,512]{1,0:T(8,128)S(1)}) custom-call(s32[14]{0:T(128)S(1)} %add_convert_fusion.valid_ref, bf16[512,640]{1,0:T(8,128)(2,1)S(1)} %get-tuple-element.39.query_ref, bf16[512,640]{1,0:T(8,128)(2,1)S(1)} %get-tuple-element.40.refs_0_, bf16[512,640]{1,0:T(8,128)(2,1)S(1)} %get-tuple-element.38.ranked_value_ref.refs_1_), custom_call_target="tpu_custom_call" | custom-call | flops 671088640 | bytes 4587520 | tf_op jit(solution)/shard_map/pallas_call | solution.py:261
  32.5 0.0 collective-permute-done.2.refs_1_.refs_2_
  32.6 0.0 collective-permute-done.3.refs_1_.refs_3_
  32.6 1.9 %collective-permute-start.7 = (bf16[512,640]{1,0:T(8,128)(2,1)S(1)}, bf16[512,640]{1,0:T(8,128)(2,1)S(1)}, u32[]{:S(2)}, u32[]{:S(2)}) collective-permute-start(bf16[512,640]{1,0:T(8,128)(2,1)S(1)} %get-tuple-element.51), channel_id=1, source_target_pairs={{3,0},{4,1},{5,2},{6,3},{7,4},{8,5},{9,6},{10,7},{11,8},{12,9},{13... | collective-permute-start | bytes 1966088 | tf_op jit(solution)/shard_map/ppermute | solution.py:21
  34.5 5.1 %collective-permute-start.6 = (bf16[512,640]{1,0:T(8,128)(2,1)S(1)}, bf16[512,640]{1,0:T(8,128)(2,1)S(1)}, u32[]{:S(2)}, u32[]{:S(2)}) collective-permute-start(bf16[512,640]{1,0:T(8,128)(2,1)S(1)} %get-tuple-element.51), channel_id=1, source_target_pairs={{0,3},{1,4},{2,5},{3,6},{4,7},{5,8},{6,9},{7,10},{8,11},{9,12},{10... | collective-permute-start | bytes 1966088 | tf_op jit(solution)/shard_map/ppermute | solution.py:21
  39.6 7.5 %collective-permute-start.8 = (bf16[256,640]{1,0:T(8,128)(2,1)S(1)}, bf16[256,640]{1,0:T(8,128)(2,1)S(1)}, u32[]{:S(2)}, u32[]{:S(2)}) collective-permute-start(bf16[256,640]{1,0:T(8,128)(2,1)S(1)} %get-tuple-element.52), channel_id=1, source_target_pairs={{0,4},{1,5},{2,6},{3,7},{4,8},{5,9},{6,10},{7,11},{8,12},{9,13},{1... | collective-permute-start | bytes 983048 | tf_op jit(solution)/shard_map/ppermute | solution.py:21
  47.1 0.0 collective-permute-done.refs_0_
  47.1 9.4 %collective-permute-done.1.refs_0_.refs_1_ = bf16[512,640]{1,0:T(8,128)(2,1)S(1)} collective-permute-done((bf16[512,640]{1,0:T(8,128)(2,1)S(1)}, bf16[512,640]{1,0:T(8,128)(2,1)S(1)}, u32[]{:S(2)}, u32[]{:S(2)}) %collective-permute-start.1) | collective-permute-done | bytes 655392 | tf_op jit(solution)/shard_map/ppermute | solution.py:21
  56.5 0.2 shard_map.68
  56.8 3.6 %collective-permute-start.5 = (bf16[512,640]{1,0:T(8,128)(2,1)S(1)}, bf16[512,640]{1,0:T(8,128)(2,1)S(1)}, u32[]{:S(2)}, u32[]{:S(2)}) collective-permute-start(bf16[512,640]{1,0:T(8,128)(2,1)S(1)} %shard_map.68), channel_id=1, source_target_pairs={{1,0},{2,1},{3,2},{4,3},{5,4},{6,5},{7,6},{8,7},{9,8},{10,9},{11,1... | collective-permute-start | bytes 1966088 | tf_op jit(solution)/shard_map/ppermute | solution.py:21
  60.3 0.2 shard_map.67
  60.6 2.3 %collective-permute-start.4 = (bf16[512,640]{1,0:T(8,128)(2,1)S(1)}, bf16[512,640]{1,0:T(8,128)(2,1)S(1)}, u32[]{:S(2)}, u32[]{:S(2)}) collective-permute-start(bf16[512,640]{1,0:T(8,128)(2,1)S(1)} %shard_map.67), channel_id=1, source_target_pairs={{0,1},{1,2},{2,3},{3,4},{4,5},{5,6},{6,7},{7,8},{8,9},{9,10},{10,1... | collective-permute-start | bytes 1966088 | tf_op jit(solution)/shard_map/ppermute | solution.py:21
  62.8 0.0 collective-permute-done.7.refs_2_.refs_1_
  62.9 2.0 %collective-permute-start.9 = (bf16[256,640]{1,0:T(8,128)(2,1)S(1)}, bf16[256,640]{1,0:T(8,128)(2,1)S(1)}, u32[]{:S(2)}, u32[]{:S(2)}) collective-permute-start(bf16[256,640]{1,0:T(8,128)(2,1)S(1)} %get-tuple-element.52), channel_id=1, source_target_pairs={{4,0},{5,1},{6,2},{7,3},{8,4},{9,5},{10,6},{11,7},{12,8},{13,9},{1... | collective-permute-start | bytes 983048 | tf_op jit(solution)/shard_map/ppermute | solution.py:21
  64.9 0.9 shard_map.70
  65.8 0.0 collective-permute-done.6.refs_2_.refs_0_
  65.8 2.0 %collective-permute-start.13 = (bf16[512,640]{1,0:T(8,128)(2,1)S(1)}, bf16[512,640]{1,0:T(8,128)(2,1)S(1)}, u32[]{:S(2)}, u32[]{:S(2)}) collective-permute-start(bf16[512,640]{1,0:T(8,128)(2,1)S(1)} %shard_map.70), channel_id=1, source_target_pairs={{4,0},{5,1},{6,2},{7,3},{8,4},{9,5},{10,6},{11,7},{12,8},{13,9},{1... | collective-permute-start | bytes 1966088 | tf_op jit(solution)/shard_map/ppermute | solution.py:21
  67.8 0.9 shard_map.69
  68.7 0.0 collective-permute-done.8.refs_2_
  68.7 6.9 %collective-permute-start.12 = (bf16[512,640]{1,0:T(8,128)(2,1)S(1)}, bf16[512,640]{1,0:T(8,128)(2,1)S(1)}, u32[]{:S(2)}, u32[]{:S(2)}) collective-permute-start(bf16[512,640]{1,0:T(8,128)(2,1)S(1)} %shard_map.69), channel_id=1, source_target_pairs={{0,4},{1,5},{2,6},{3,7},{4,8},{5,9},{6,10},{7,11},{8,12},{9,13},{1... | collective-permute-start | bytes 1966088 | tf_op jit(solution)/shard_map/ppermute | solution.py:21
  75.6 4.4 %shard_map.71 = (f32[640,512]{1,0:T(8,128)S(1)}, f32[16,512]{1,0:T(8,128)S(1)}) custom-call(s32[14]{0:T(128)S(1)} %add_convert_fusion.valid_ref, bf16[512,640]{1,0:T(8,128)(2,1)S(1)} %get-tuple-element.39.query_ref, bf16[512,640]{1,0:T(8,128)(2,1)S(1)} %collective-permute-done.refs_0_, ...), custom_call_target="tpu_custom_call", output_to_operand_aliasing={{0}: (6, {}), {1}: (7, {})} | custom-call | flops 1342177280 | bytes 5898240 | tf_op jit(solution)/shard_map/pallas_call | solution.py:261
  80.0 8.5 %collective-permute-done.9.refs_3_ = bf16[256,640]{1,0:T(8,128)(2,1)S(1)} collective-permute-done((bf16[256,640]{1,0:T(8,128)(2,1)S(1)}, bf16[256,640]{1,0:T(8,128)(2,1)S(1)}, u32[]{:S(2)}, u32[]{:S(2)}) %collective-permute-start.9) | collective-permute-done | bytes 327712 | tf_op jit(solution)/shard_map/ppermute | solution.py:21
  88.5 3.7 %shard_map.72 = (f32[640,512]{1,0:T(8,128)S(1)}, f32[16,512]{1,0:T(8,128)S(1)}) custom-call(s32[14]{0:T(128)S(1)} %add_convert_fusion.valid_ref, bf16[512,640]{1,0:T(8,128)(2,1)S(1)} %get-tuple-element.39.query_ref, bf16[512,640]{1,0:T(8,128)(2,1)S(1)} %collective-permute-done.6.refs_2_.refs_0_, ...), custom_call_target="tpu_custom_call", output_to_operand_aliasing={{0}: (6, {}), {1}: (7, {})} | custom-call | flops 1006632960 | bytes 5242880 | tf_op jit(solution)/shard_map/pallas_call | solution.py:261
  92.3 0.0 collective-permute-done.5.refs_0_.refs_1_
  92.3 0.0 collective-permute-done.4.refs_0_
  92.3 0.4 shard_map.73
  92.7 1.9 %collective-permute-start.10 = (bf16[256,640]{1,0:T(8,128)(2,1)S(1)}, bf16[256,640]{1,0:T(8,128)(2,1)S(1)}, u32[]{:S(2)}, u32[]{:S(2)}) collective-permute-start(bf16[256,640]{1,0:T(8,128)(2,1)S(1)} %shard_map.73), channel_id=1, source_target_pairs={{0,4},{1,5},{2,6},{3,7},{4,8},{5,9},{6,10},{7,11},{8,12},{9,13},{1... | collective-permute-start | bytes 983048 | tf_op jit(solution)/shard_map/ppermute | solution.py:21
  94.7 0.4 shard_map.74
  95.1 4.1 %collective-permute-start.11 = (bf16[256,640]{1,0:T(8,128)(2,1)S(1)}, bf16[256,640]{1,0:T(8,128)(2,1)S(1)}, u32[]{:S(2)}, u32[]{:S(2)}) collective-permute-start(bf16[256,640]{1,0:T(8,128)(2,1)S(1)} %shard_map.74), channel_id=1, source_target_pairs={{4,0},{5,1},{6,2},{7,3},{8,4},{9,5},{10,6},{11,7},{12,8},{13,9},{1... | collective-permute-start | bytes 983048 | tf_op jit(solution)/shard_map/ppermute | solution.py:21
  99.2 2.8 %shard_map.75 = (f32[640,512]{1,0:T(8,128)S(1)}, f32[16,512]{1,0:T(8,128)S(1)}) custom-call(s32[14]{0:T(128)S(1)} %add_convert_fusion.valid_ref, bf16[512,640]{1,0:T(8,128)(2,1)S(1)} %get-tuple-element.39.query_ref, bf16[512,640]{1,0:T(8,128)(2,1)S(1)} %collective-permute-done.4.refs_0_, ...), custom_call_target="tpu_custom_call", output_to_operand_aliasing={{0}: (4, {}), {1}: (5, {})} | custom-call | flops 671088640 | bytes 4587520 | tf_op jit(solution)/shard_map/pallas_call | solution.py:261
  102.0 0.5 collective-permute-done.13.refs_1_
  102.6 0.0 collective-permute-done.12.refs_0_
  102.6 2.8 %shard_map.76 = (f32[640,512]{1,0:T(8,128)S(1)}, f32[16,512]{1,0:T(8,128)S(1)}) custom-call(s32[14]{0:T(128)S(1)} %add_convert_fusion.valid_ref, bf16[512,640]{1,0:T(8,128)(2,1)S(1)} %get-tuple-element.39.query_ref, bf16[512,640]{1,0:T(8,128)(2,1)S(1)} %collective-permute-done.12.refs_0_, ...), custom_call_target="tpu_custom_call", output_to_operand_aliasing={{0}: (4, {}), {1}: (5, {})} | custom-call | flops 671088640 | bytes 4587520 | tf_op jit(solution)/shard_map/pallas_call | solution.py:261
  105.3 0.0 collective-permute-done.10.refs_0_
  105.4 2.4 %collective-permute-done.11.refs_1_ = bf16[256,640]{1,0:T(8,128)(2,1)S(1)} collective-permute-done((bf16[256,640]{1,0:T(8,128)(2,1)S(1)}, bf16[256,640]{1,0:T(8,128)(2,1)S(1)}, u32[]{:S(2)}, u32[]{:S(2)}) %collective-permute-start.11) | collective-permute-done | bytes 327712 | tf_op jit(solution)/shard_map/ppermute | solution.py:21
  107.8 3.0 %shard_map.77 = f32[512,640]{1,0:T(8,128)} custom-call(s32[14]{0:T(128)S(1)} %add_convert_fusion.valid_ref, bf16[512,640]{1,0:T(8,128)(2,1)S(1)} %get-tuple-element.39.query_ref, bf16[256,640]{1,0:T(8,128)(2,1)S(1)} %collective-permute-done.10.refs_0_, bf16[256,640]{1,0:T(8,128)(2,1)S(1)} %collective-permute-done.11.refs_1_, ...), custom_call_target="tpu_custom_call" | custom-call | flops 335544320 | bytes 3932160 | tf_op jit(solution)/shard_map/pallas_call | solution.py:261
  (3 shorter events, 0.0 us)
Async XLA Ops:
  0.0 20.2 %copy-start.2 = (s32[1,16]{1,0:T(1,128)S(1)}, s32[1,16]{1,0:T(1,128)}, u32[]{:S(2)}) copy-start(s32[1,16]{1,0:T(1,128)} %blocks_ref.1) | copy-start | bytes 196
  0.0 20.2 %copy-start = (bf16[512,640]{1,0:T(8,128)(2,1)S(1)}, bf16[512,640]{1,0:T(8,128)(2,1)}, u32[]{:S(2)}) copy-start(bf16[512,640]{1,0:T(8,128)(2,1)} %query_hbm.3) | copy-start | bytes 1966084
  0.0 20.2 %copy-start.1 = (bf16[512,640]{1,0:T(8,128)(2,1)S(1)}, bf16[512,640]{1,0:T(8,128)(2,1)}, u32[]{:S(2)}) copy-start(bf16[512,640]{1,0:T(8,128)(2,1)} %key_hbm.3) | copy-start | bytes 1966084
  0.0 14.8 %copy-start.3 = (f32[640]{0:T(1024)S(1)}, f32[640]{0:T(1024)}, u32[]{:S(2)}) copy-start(f32[640]{0:T(1024)} %param.9) | copy-start | bytes 7684
  0.0 14.8 %copy-start.4 = (f32[640]{0:T(1024)S(1)}, f32[640]{0:T(1024)}, u32[]{:S(2)}) copy-start(f32[640]{0:T(1024)} %param.10) | copy-start | bytes 7684
  2.5 30.1 %collective-permute-start.2 = (bf16[512,640]{1,0:T(8,128)(2,1)S(1)}, bf16[512,640]{1,0:T(8,128)(2,1)S(1)}, u32[]{:S(2)}, u32[]{:S(2)}) collective-permute-start(bf16[512,640]{1,0:T(8,128)(2,1)S(1)} %get-tuple-element.38.ranked_value_ref.refs_1_), channel_id=1, source_target_pairs={{0,1},{1,2},{2,3},{3,4},{4,5},{5,6},{6,7},{7,8},{8,9},{9,10},{10,1... | collective-permute-start | bytes 1966088 | tf_op jit(solution)/shard_map/ppermute | solution.py:21
  6.0 26.6 %collective-permute-start.3 = (bf16[512,640]{1,0:T(8,128)(2,1)S(1)}, bf16[512,640]{1,0:T(8,128)(2,1)S(1)}, u32[]{:S(2)}, u32[]{:S(2)}) collective-permute-start(bf16[512,640]{1,0:T(8,128)(2,1)S(1)} %get-tuple-element.38.ranked_value_ref.refs_1_), channel_id=1, source_target_pairs={{1,0},{2,1},{3,2},{4,3},{5,4},{6,5},{7,6},{8,7},{9,8},{10,9},{11,1... | collective-permute-start | bytes 1966088 | tf_op jit(solution)/shard_map/ppermute | solution.py:21
  10.4 9.8 %all-to-all-start = ((f32[8,2,512]{2,1,0:T(2,128)}), f32[8,2,512]{2,1,0:T(2,128)S(1)}, u32[]{:S(2)}, u32[]{:S(2)}) async-start(f32[8,2,512]{2,1,0:T(2,128)} %get-tuple-element.37), calls=%async_computation | async-start | bytes 65536 | tf_op jit(solution)/shard_map/all_to_all | solution.py:306
  21.9 25.2 %collective-permute-start = (bf16[512,640]{1,0:T(8,128)(2,1)S(1)}, bf16[512,640]{1,0:T(8,128)(2,1)S(1)}, u32[]{:S(2)}, u32[]{:S(2)}) collective-permute-start(bf16[512,640]{1,0:T(8,128)(2,1)S(1)} %get-tuple-element.40.refs_0_), channel_id=1, source_target_pairs={{0,1},{1,2},{2,3},{3,4},{4,5},{5,6},{6,7},{7,8},{8,9},{9,10},{10,1... | collective-permute-start | bytes 1966088 | tf_op jit(solution)/shard_map/ppermute | solution.py:21
  23.9 32.6 %collective-permute-start.1 = (bf16[512,640]{1,0:T(8,128)(2,1)S(1)}, bf16[512,640]{1,0:T(8,128)(2,1)S(1)}, u32[]{:S(2)}, u32[]{:S(2)}) collective-permute-start(bf16[512,640]{1,0:T(8,128)(2,1)S(1)} %get-tuple-element.40.refs_0_), channel_id=1, source_target_pairs={{1,0},{2,1},{3,2},{4,3},{5,4},{6,5},{7,6},{8,7},{9,8},{10,9},{11,1... | collective-permute-start | bytes 1966088 | tf_op jit(solution)/shard_map/ppermute | solution.py:21
  32.6 30.3 %collective-permute-start.7 = (bf16[512,640]{1,0:T(8,128)(2,1)S(1)}, bf16[512,640]{1,0:T(8,128)(2,1)S(1)}, u32[]{:S(2)}, u32[]{:S(2)}) collective-permute-start(bf16[512,640]{1,0:T(8,128)(2,1)S(1)} %get-tuple-element.51), channel_id=1, source_target_pairs={{3,0},{4,1},{5,2},{6,3},{7,4},{8,5},{9,6},{10,7},{11,8},{12,9},{13... | collective-permute-start | bytes 1966088 | tf_op jit(solution)/shard_map/ppermute | solution.py:21
  34.5 31.3 %collective-permute-start.6 = (bf16[512,640]{1,0:T(8,128)(2,1)S(1)}, bf16[512,640]{1,0:T(8,128)(2,1)S(1)}, u32[]{:S(2)}, u32[]{:S(2)}) collective-permute-start(bf16[512,640]{1,0:T(8,128)(2,1)S(1)} %get-tuple-element.51), channel_id=1, source_target_pairs={{0,3},{1,4},{2,5},{3,6},{4,7},{5,8},{6,9},{7,10},{8,11},{9,12},{10... | collective-permute-start | bytes 1966088 | tf_op jit(solution)/shard_map/ppermute | solution.py:21
  39.6 29.1 %collective-permute-start.8 = (bf16[256,640]{1,0:T(8,128)(2,1)S(1)}, bf16[256,640]{1,0:T(8,128)(2,1)S(1)}, u32[]{:S(2)}, u32[]{:S(2)}) collective-permute-start(bf16[256,640]{1,0:T(8,128)(2,1)S(1)} %get-tuple-element.52), channel_id=1, source_target_pairs={{0,4},{1,5},{2,6},{3,7},{4,8},{5,9},{6,10},{7,11},{8,12},{9,13},{1... | collective-permute-start | bytes 983048 | tf_op jit(solution)/shard_map/ppermute | solution.py:21
  56.8 35.5 %collective-permute-start.5 = (bf16[512,640]{1,0:T(8,128)(2,1)S(1)}, bf16[512,640]{1,0:T(8,128)(2,1)S(1)}, u32[]{:S(2)}, u32[]{:S(2)}) collective-permute-start(bf16[512,640]{1,0:T(8,128)(2,1)S(1)} %shard_map.68), channel_id=1, source_target_pairs={{1,0},{2,1},{3,2},{4,3},{5,4},{6,5},{7,6},{8,7},{9,8},{10,9},{11,1... | collective-permute-start | bytes 1966088 | tf_op jit(solution)/shard_map/ppermute | solution.py:21
  60.6 31.7 %collective-permute-start.4 = (bf16[512,640]{1,0:T(8,128)(2,1)S(1)}, bf16[512,640]{1,0:T(8,128)(2,1)S(1)}, u32[]{:S(2)}, u32[]{:S(2)}) collective-permute-start(bf16[512,640]{1,0:T(8,128)(2,1)S(1)} %shard_map.67), channel_id=1, source_target_pairs={{0,1},{1,2},{2,3},{3,4},{4,5},{5,6},{6,7},{7,8},{8,9},{9,10},{10,1... | collective-permute-start | bytes 1966088 | tf_op jit(solution)/shard_map/ppermute | solution.py:21
  62.9 25.7 %collective-permute-start.9 = (bf16[256,640]{1,0:T(8,128)(2,1)S(1)}, bf16[256,640]{1,0:T(8,128)(2,1)S(1)}, u32[]{:S(2)}, u32[]{:S(2)}) collective-permute-start(bf16[256,640]{1,0:T(8,128)(2,1)S(1)} %get-tuple-element.52), channel_id=1, source_target_pairs={{4,0},{5,1},{6,2},{7,3},{8,4},{9,5},{10,6},{11,7},{12,8},{13,9},{1... | collective-permute-start | bytes 983048 | tf_op jit(solution)/shard_map/ppermute | solution.py:21
  65.8 36.8 %collective-permute-start.13 = (bf16[512,640]{1,0:T(8,128)(2,1)S(1)}, bf16[512,640]{1,0:T(8,128)(2,1)S(1)}, u32[]{:S(2)}, u32[]{:S(2)}) collective-permute-start(bf16[512,640]{1,0:T(8,128)(2,1)S(1)} %shard_map.70), channel_id=1, source_target_pairs={{4,0},{5,1},{6,2},{7,3},{8,4},{9,5},{10,6},{11,7},{12,8},{13,9},{1... | collective-permute-start | bytes 1966088 | tf_op jit(solution)/shard_map/ppermute | solution.py:21
  68.7 33.8 %collective-permute-start.12 = (bf16[512,640]{1,0:T(8,128)(2,1)S(1)}, bf16[512,640]{1,0:T(8,128)(2,1)S(1)}, u32[]{:S(2)}, u32[]{:S(2)}) collective-permute-start(bf16[512,640]{1,0:T(8,128)(2,1)S(1)} %shard_map.69), channel_id=1, source_target_pairs={{0,4},{1,5},{2,6},{3,7},{4,8},{5,9},{6,10},{7,11},{8,12},{9,13},{1... | collective-permute-start | bytes 1966088 | tf_op jit(solution)/shard_map/ppermute | solution.py:21
  92.7 12.6 %collective-permute-start.10 = (bf16[256,640]{1,0:T(8,128)(2,1)S(1)}, bf16[256,640]{1,0:T(8,128)(2,1)S(1)}, u32[]{:S(2)}, u32[]{:S(2)}) collective-permute-start(bf16[256,640]{1,0:T(8,128)(2,1)S(1)} %shard_map.73), channel_id=1, source_target_pairs={{0,4},{1,5},{2,6},{3,7},{4,8},{5,9},{6,10},{7,11},{8,12},{9,13},{1... | collective-permute-start | bytes 983048 | tf_op jit(solution)/shard_map/ppermute | solution.py:21
  95.1 12.7 %collective-permute-start.11 = (bf16[256,640]{1,0:T(8,128)(2,1)S(1)}, bf16[256,640]{1,0:T(8,128)(2,1)S(1)}, u32[]{:S(2)}, u32[]{:S(2)}) collective-permute-start(bf16[256,640]{1,0:T(8,128)(2,1)S(1)} %shard_map.74), channel_id=1, source_target_pairs={{4,0},{5,1},{6,2},{7,3},{8,4},{9,5},{10,6},{11,7},{12,8},{13,9},{1... | collective-permute-start | bytes 983048 | tf_op jit(solution)/shard_map/ppermute | solution.py:21

commit v4 on v3

--- a/solution.py
+++ b/solution.py
@@ -376,21 +376,15 @@
         valid,
         state,
     )
-    state = attend(
+    return attend(
         query,
-        far,
+        [*far, *sixth],
         [
             (side, place * quarter, side, (2 + place) * quarter, quarter, flag(side, steps))
             for side in sides
             for place, steps in enumerate((5, 7))
-        ],
-        valid,
-        state,
-    )
-    return attend(
-        query,
-        sixth,
-        [(side, 0, side, quarter, quarter, flag(side, 6)) for side in sides],
+        ]
+        + [(2 + side, 0, 2 + side, quarter, quarter, flag(side, 6)) for side in sides],
         valid,
         state,
         last=True,

time: 111 us -> 121 us (1.090)
  the two profiles are of different devices: /device:TPU:224 before, /device:TPU:184 now
where the time goes in v4:
time: 121 us; the launch traced here: 120 us
  starting transfers between devices  55.3 us (46%)
  waiting for transfers between devices  39 us (32%)
  Pallas kernels  25.4 us (21%)
    ppermute x14, starting transfers between devices, shift(): lax.ppermute(value, 'frames', [(source, source + steps) for source in ran...  51 us
    ppermute x14, waiting for transfers between devices, shift(): lax.ppermute(value, 'frames', [(source, source + steps) for source in ran...  33.6 us
    pallas_call x5, Pallas kernels, attend(): pl.pallas_call(functools.partial(attend_kernel, pieces, first, last, len(...  18.1 us
    all_to_all x1, waiting for transfers between devices, on_device(): squares = lax.all_to_all(squares, 'heads', 0, 0)  5.41 us
    all_to_all x1, starting transfers between devices, on_device(): squares = lax.all_to_all(squares, 'heads', 0, 0)  4.31 us
    pallas_call x6, Pallas kernels, pack(): pl.pallas_call(functools.partial(pack_kernel, parts), out_shape=jax.Shape...  3.11 us
    pallas_call x1, Pallas kernels, on_device(): pl.pallas_call(gather_kernel, out_shape=(block, jax.ShapeDtypeStruct((dev...  2.44 us
  transfers between devices with their start and end apart: 15, of which 6 were waited for; matrix products, arithmetic and copies ran while one was open for 0% of the time, Pallas kernels for 15%

profile of v4, /device:TPU:184, one launch (start us, length us, event | category | flops | bytes accessed | tf_op | source)
XLA Modules:
  0.0 120.1 jit_solution(8297771788535500659)
XLA Ops:
  0.0 0.0 copy-start.2
  0.0 0.0 copy-start
  0.0 0.0 copy-start.1
  0.0 0.0 copy-start.3
  0.0 0.0 copy-start.4
  0.0 2.4 %shard_map.64 = (bf16[512,640]{1,0:T(8,128)(2,1)S(1)}, f32[8,2,512]{2,1,0:T(2,128)}) custom-call(s32[1,16]{1,0:T(1,128)} %blocks_ref.1, bf16[512,640]{1,0:T(8,128)(2,1)} %query_hbm.3, bf16[512,640]{1,0:T(8,128)(2,1)} %key_hbm.3, bf16[512,640]{1,0:T(8,128)(2,1)} %value_hbm.1), custom_call_target="tpu_custom_call" | custom-call | flops 1310720 | bytes 2621440 | tf_op jit(solution)/shard_map/pallas_call | solution.py:289
  2.5 3.5 %collective-permute-start.2 = (bf16[512,640]{1,0:T(8,128)(2,1)S(1)}, bf16[512,640]{1,0:T(8,128)(2,1)S(1)}, u32[]{:S(2)}, u32[]{:S(2)}) collective-permute-start(bf16[512,640]{1,0:T(8,128)(2,1)S(1)} %get-tuple-element.36.ranked_value_ref.refs_1_), channel_id=1, source_target_pairs={{0,1},{1,2},{2,3},{3,4},{4,5},{5,6},{6,7},{7,8},{8,9},{9,10},{10,1... | collective-permute-start | bytes 1966088 | tf_op jit(solution)/shard_map/ppermute | solution.py:21
  6.0 2.4 %collective-permute-start.3 = (bf16[512,640]{1,0:T(8,128)(2,1)S(1)}, bf16[512,640]{1,0:T(8,128)(2,1)S(1)}, u32[]{:S(2)}, u32[]{:S(2)}) collective-permute-start(bf16[512,640]{1,0:T(8,128)(2,1)S(1)} %get-tuple-element.36.ranked_value_ref.refs_1_), channel_id=1, source_target_pairs={{1,0},{2,1},{3,2},{4,3},{5,4},{6,5},{7,6},{8,7},{9,8},{10,9},{11,1... | collective-permute-start | bytes 1966088 | tf_op jit(solution)/shard_map/ppermute | solution.py:21
  8.3 4.3 %all-to-all-start = ((f32[8,2,512]{2,1,0:T(2,128)}), f32[8,2,512]{2,1,0:T(2,128)S(1)}, u32[]{:S(2)}, u32[]{:S(2)}) async-start(f32[8,2,512]{2,1,0:T(2,128)} %get-tuple-element.35), calls=%async_computation | async-start | bytes 65536 | tf_op jit(solution)/shard_map/all_to_all | solution.py:306
  12.7 0.0 copy-done.3
  12.7 0.0 copy-done.4
  12.7 5.4 %all-to-all-done.squares_ref = f32[8,2,512]{2,1,0:T(2,128)S(1)} async-done(((f32[8,2,512]{2,1,0:T(2,128)}), f32[8,2,512]{2,1,0:T(2,128)S(1)}, u32[]{:S(2)}, u32[]{:S(2)}) %all-to-all-start) | async-done | bytes 32800 | tf_op jit(solution)/shard_map/all_to_all | solution.py:306
  18.1 0.0 copy-done.2
  18.1 0.0 copy-done
  18.1 0.0 copy-done.1
  18.1 1.7 %shard_map.65 = (bf16[512,640]{1,0:T(8,128)(2,1)S(1)}, bf16[512,640]{1,0:T(8,128)(2,1)S(1)}, bf16[512,640]{1,0:T(8,128)(2,1)S(1)}, bf16[256,640]{1,0:T(8,128)(2,1)S(1)}) custom-call(s32[1,16]{1,0:T(1,128)S(1)} %copy-done.2, f32[8,2,512]{2,1,0:T(2,128)S(1)} %all-to-all-done.squares_ref, f32[1,640]{1,0:T(1,128)S(1)} %reshape.6.query_gain_ref, ...), custom_call_target="tpu_custom_call" | custom-call | flops 1966080 | bytes 3932160 | tf_op jit(solution)/shard_map/pallas_call | solution.py:308
  19.8 5.6 %collective-permute-start = (bf16[512,640]{1,0:T(8,128)(2,1)S(1)}, bf16[512,640]{1,0:T(8,128)(2,1)S(1)}, u32[]{:S(2)}, u32[]{:S(2)}) collective-permute-start(bf16[512,640]{1,0:T(8,128)(2,1)S(1)} %get-tuple-element.38.refs_0_), channel_id=1, source_target_pairs={{0,1},{1,2},{2,3},{3,4},{4,5},{5,6},{6,7},{7,8},{8,9},{9,10},{10,1... | collective-permute-start | bytes 1966088 | tf_op jit(solution)/shard_map/ppermute | solution.py:21
  25.4 1.9 %collective-permute-start.1 = (bf16[512,640]{1,0:T(8,128)(2,1)S(1)}, bf16[512,640]{1,0:T(8,128)(2,1)S(1)}, u32[]{:S(2)}, u32[]{:S(2)}) collective-permute-start(bf16[512,640]{1,0:T(8,128)(2,1)S(1)} %get-tuple-element.38.refs_0_), channel_id=1, source_target_pairs={{1,0},{2,1},{3,2},{4,3},{5,4},{6,5},{7,6},{8,7},{9,8},{10,9},{11,1... | collective-permute-start | bytes 1966088 | tf_op jit(solution)/shard_map/ppermute | solution.py:21
  27.4 0.1 add_convert_fusion.valid_ref
  27.5 2.6 %shard_map.66 = (f32[640,512]{1,0:T(8,128)S(1)}, f32[16,512]{1,0:T(8,128)S(1)}) custom-call(s32[14]{0:T(128)S(1)} %add_convert_fusion.valid_ref, bf16[512,640]{1,0:T(8,128)(2,1)S(1)} %get-tuple-element.37.query_ref, bf16[512,640]{1,0:T(8,128)(2,1)S(1)} %get-tuple-element.38.refs_0_, bf16[512,640]{1,0:T(8,128)(2,1)S(1)} %get-tuple-element.36.ranked_value_ref.refs_1_), custom_call_target="tpu_custom_call" | custom-call | flops 671088640 | bytes 4587520 | tf_op jit(solution)/shard_map/pallas_call | solution.py:261
  30.0 0.0 collective-permute-done.2.refs_1_.refs_2_
  30.0 0.0 collective-permute-done.3.refs_1_.refs_3_
  30.0 4.7 %collective-permute-start.6 = (bf16[512,640]{1,0:T(8,128)(2,1)S(1)}, bf16[512,640]{1,0:T(8,128)(2,1)S(1)}, u32[]{:S(2)}, u32[]{:S(2)}) collective-permute-start(bf16[512,640]{1,0:T(8,128)(2,1)S(1)} %get-tuple-element.47), channel_id=1, source_target_pairs={{3,0},{4,1},{5,2},{6,3},{7,4},{8,5},{9,6},{10,7},{11,8},{12,9},{13... | collective-permute-start | bytes 1966088 | tf_op jit(solution)/shard_map/ppermute | solution.py:21
  34.7 2.1 %collective-permute-start.4 = (bf16[512,640]{1,0:T(8,128)(2,1)S(1)}, bf16[512,640]{1,0:T(8,128)(2,1)S(1)}, u32[]{:S(2)}, u32[]{:S(2)}) collective-permute-start(bf16[512,640]{1,0:T(8,128)(2,1)S(1)} %get-tuple-element.47), channel_id=1, source_target_pairs={{0,3},{1,4},{2,5},{3,6},{4,7},{5,8},{6,9},{7,10},{8,11},{9,12},{10... | collective-permute-start | bytes 1966088 | tf_op jit(solution)/shard_map/ppermute | solution.py:21
  36.8 15.7 %collective-permute-done.refs_0_ = bf16[512,640]{1,0:T(8,128)(2,1)S(1)} collective-permute-done((bf16[512,640]{1,0:T(8,128)(2,1)S(1)}, bf16[512,640]{1,0:T(8,128)(2,1)S(1)}, u32[]{:S(2)}, u32[]{:S(2)}) %collective-permute-start) | collective-permute-done | bytes 655392 | tf_op jit(solution)/shard_map/ppermute | solution.py:21
  52.5 3.1 %collective-permute-done.1.refs_0_.refs_1_ = bf16[512,640]{1,0:T(8,128)(2,1)S(1)} collective-permute-done((bf16[512,640]{1,0:T(8,128)(2,1)S(1)}, bf16[512,640]{1,0:T(8,128)(2,1)S(1)}, u32[]{:S(2)}, u32[]{:S(2)}) %collective-permute-start.1) | collective-permute-done | bytes 655392 | tf_op jit(solution)/shard_map/ppermute | solution.py:21
  55.6 0.2 shard_map.70
  55.8 4.4 %collective-permute-start.9 = (bf16[512,640]{1,0:T(8,128)(2,1)S(1)}, bf16[512,640]{1,0:T(8,128)(2,1)S(1)}, u32[]{:S(2)}, u32[]{:S(2)}) collective-permute-start(bf16[512,640]{1,0:T(8,128)(2,1)S(1)} %shard_map.70), channel_id=1, source_target_pairs={{1,0},{2,1},{3,2},{4,3},{5,4},{6,5},{7,6},{8,7},{9,8},{10,9},{11,1... | collective-permute-start | bytes 1966088 | tf_op jit(solution)/shard_map/ppermute | solution.py:21
  60.2 0.2 shard_map.69
  60.5 3.6 %collective-permute-start.8 = (bf16[512,640]{1,0:T(8,128)(2,1)S(1)}, bf16[512,640]{1,0:T(8,128)(2,1)S(1)}, u32[]{:S(2)}, u32[]{:S(2)}) collective-permute-start(bf16[512,640]{1,0:T(8,128)(2,1)S(1)} %shard_map.69), channel_id=1, source_target_pairs={{0,1},{1,2},{2,3},{3,4},{4,5},{5,6},{6,7},{7,8},{8,9},{9,10},{10,1... | collective-permute-start | bytes 1966088 | tf_op jit(solution)/shard_map/ppermute | solution.py:21
  64.0 3.8 %collective-permute-start.10 = (bf16[256,640]{1,0:T(8,128)(2,1)S(1)}, bf16[256,640]{1,0:T(8,128)(2,1)S(1)}, u32[]{:S(2)}, u32[]{:S(2)}) collective-permute-start(bf16[256,640]{1,0:T(8,128)(2,1)S(1)} %get-tuple-element.50), channel_id=1, source_target_pairs={{0,4},{1,5},{2,6},{3,7},{4,8},{5,9},{6,10},{7,11},{8,12},{9,13},{1... | collective-permute-start | bytes 983048 | tf_op jit(solution)/shard_map/ppermute | solution.py:21
  67.9 0.0 collective-permute-done.6.refs_2_.refs_1_
  67.9 2.0 %collective-permute-start.11 = (bf16[256,640]{1,0:T(8,128)(2,1)S(1)}, bf16[256,640]{1,0:T(8,128)(2,1)S(1)}, u32[]{:S(2)}, u32[]{:S(2)}) collective-permute-start(bf16[256,640]{1,0:T(8,128)(2,1)S(1)} %get-tuple-element.50), channel_id=1, source_target_pairs={{4,0},{5,1},{6,2},{7,3},{8,4},{9,5},{10,6},{11,7},{12,8},{13,9},{1... | collective-permute-start | bytes 983048 | tf_op jit(solution)/shard_map/ppermute | solution.py:21
  69.9 0.9 shard_map.68
  70.8 0.0 collective-permute-done.4.refs_2_.refs_0_
  70.8 3.7 %collective-permute-start.7 = (bf16[512,640]{1,0:T(8,128)(2,1)S(1)}, bf16[512,640]{1,0:T(8,128)(2,1)S(1)}, u32[]{:S(2)}, u32[]{:S(2)}) collective-permute-start(bf16[512,640]{1,0:T(8,128)(2,1)S(1)} %shard_map.68), channel_id=1, source_target_pairs={{4,0},{5,1},{6,2},{7,3},{8,4},{9,5},{10,6},{11,7},{12,8},{13,9},{1... | collective-permute-start | bytes 1966088 | tf_op jit(solution)/shard_map/ppermute | solution.py:21
  74.6 0.9 shard_map.67
  75.5 8.7 %collective-permute-done.10.refs_2_ = bf16[256,640]{1,0:T(8,128)(2,1)S(1)} collective-permute-done((bf16[256,640]{1,0:T(8,128)(2,1)S(1)}, bf16[256,640]{1,0:T(8,128)(2,1)S(1)}, u32[]{:S(2)}, u32[]{:S(2)}) %collective-permute-start.10) | collective-permute-done | bytes 327712 | tf_op jit(solution)/shard_map/ppermute | solution.py:21
  84.2 4.4 %collective-permute-start.5 = (bf16[512,640]{1,0:T(8,128)(2,1)S(1)}, bf16[512,640]{1,0:T(8,128)(2,1)S(1)}, u32[]{:S(2)}, u32[]{:S(2)}) collective-permute-start(bf16[512,640]{1,0:T(8,128)(2,1)S(1)} %shard_map.67), channel_id=1, source_target_pairs={{0,4},{1,5},{2,6},{3,7},{4,8},{5,9},{6,10},{7,11},{8,12},{9,13},{1... | collective-permute-start | bytes 1966088 | tf_op jit(solution)/shard_map/ppermute | solution.py:21
  88.5 4.4 %shard_map.71 = (f32[640,512]{1,0:T(8,128)S(1)}, f32[16,512]{1,0:T(8,128)S(1)}) custom-call(s32[14]{0:T(128)S(1)} %add_convert_fusion.valid_ref, bf16[512,640]{1,0:T(8,128)(2,1)S(1)} %get-tuple-element.37.query_ref, bf16[512,640]{1,0:T(8,128)(2,1)S(1)} %collective-permute-done.refs_0_, ...), custom_call_target="tpu_custom_call", output_to_operand_aliasing={{0}: (6, {}), {1}: (7, {})} | custom-call | flops 1342177280 | bytes 5898240 | tf_op jit(solution)/shard_map/pallas_call | solution.py:261
  92.9 0.0 collective-permute-done.11.refs_3_
  92.9 3.7 %shard_map.72 = (f32[640,512]{1,0:T(8,128)S(1)}, f32[16,512]{1,0:T(8,128)S(1)}) custom-call(s32[14]{0:T(128)S(1)} %add_convert_fusion.valid_ref, bf16[512,640]{1,0:T(8,128)(2,1)S(1)} %get-tuple-element.37.query_ref, bf16[512,640]{1,0:T(8,128)(2,1)S(1)} %collective-permute-done.4.refs_2_.refs_0_, ...), custom_call_target="tpu_custom_call", output_to_operand_aliasing={{0}: (6, {}), {1}: (7, {})} | custom-call | flops 1006632960 | bytes 5242880 | tf_op jit(solution)/shard_map/pallas_call | solution.py:261
  96.7 0.0 collective-permute-done.9.refs_0_.refs_1_
  96.7 0.0 collective-permute-done.8.refs_0_
  96.7 0.4 shard_map.73
  97.2 6.9 %collective-permute-start.12 = (bf16[256,640]{1,0:T(8,128)(2,1)S(1)}, bf16[256,640]{1,0:T(8,128)(2,1)S(1)}, u32[]{:S(2)}, u32[]{:S(2)}) collective-permute-start(bf16[256,640]{1,0:T(8,128)(2,1)S(1)} %shard_map.73), channel_id=1, source_target_pairs={{0,4},{1,5},{2,6},{3,7},{4,8},{5,9},{6,10},{7,11},{8,12},{9,13},{1... | collective-permute-start | bytes 983048 | tf_op jit(solution)/shard_map/ppermute | solution.py:21
  104.0 0.4 shard_map.74
  104.5 2.1 %collective-permute-start.13 = (bf16[256,640]{1,0:T(8,128)(2,1)S(1)}, bf16[256,640]{1,0:T(8,128)(2,1)S(1)}, u32[]{:S(2)}, u32[]{:S(2)}) collective-permute-start(bf16[256,640]{1,0:T(8,128)(2,1)S(1)} %shard_map.74), channel_id=1, source_target_pairs={{4,0},{5,1},{6,2},{7,3},{8,4},{9,5},{10,6},{11,7},{12,8},{13,9},{1... | collective-permute-start | bytes 983048 | tf_op jit(solution)/shard_map/ppermute | solution.py:21
  106.6 2.8 %shard_map.75 = (f32[640,512]{1,0:T(8,128)S(1)}, f32[16,512]{1,0:T(8,128)S(1)}) custom-call(s32[14]{0:T(128)S(1)} %add_convert_fusion.valid_ref, bf16[512,640]{1,0:T(8,128)(2,1)S(1)} %get-tuple-element.37.query_ref, bf16[512,640]{1,0:T(8,128)(2,1)S(1)} %collective-permute-done.8.refs_0_, ...), custom_call_target="tpu_custom_call", output_to_operand_aliasing={{0}: (4, {}), {1}: (5, {})} | custom-call | flops 671088640 | bytes 4587520 | tf_op jit(solution)/shard_map/pallas_call | solution.py:261
  109.4 0.9 collective-permute-done.12.refs_2_
  110.3 5.1 %collective-permute-done.13.refs_3_ = bf16[256,640]{1,0:T(8,128)(2,1)S(1)} collective-permute-done((bf16[256,640]{1,0:T(8,128)(2,1)S(1)}, bf16[256,640]{1,0:T(8,128)(2,1)S(1)}, u32[]{:S(2)}, u32[]{:S(2)}) %collective-permute-start.13) | collective-permute-done | bytes 327712 | tf_op jit(solution)/shard_map/ppermute | solution.py:21
  115.4 0.0 collective-permute-done.7.refs_1_
  115.4 0.0 collective-permute-done.5.refs_0_
  115.4 4.6 %shard_map.76 = f32[512,640]{1,0:T(8,128)} custom-call(s32[14]{0:T(128)S(1)} %add_convert_fusion.valid_ref, bf16[512,640]{1,0:T(8,128)(2,1)S(1)} %get-tuple-element.37.query_ref, bf16[512,640]{1,0:T(8,128)(2,1)S(1)} %collective-permute-done.5.refs_0_, bf16[512,640]{1,0:T(8,128)(2,1)S(1)} %collective-permute-done.7.refs_1_, ...), custom_call_target="tpu_custom_call" | custom-call | flops 1006632960 | bytes 5242880 | tf_op jit(solution)/shard_map/pallas_call | solution.py:261
  (3 shorter events, 0.0 us)
Async XLA Ops:
  0.0 18.1 %copy-start.2 = (s32[1,16]{1,0:T(1,128)S(1)}, s32[1,16]{1,0:T(1,128)}, u32[]{:S(2)}) copy-start(s32[1,16]{1,0:T(1,128)} %blocks_ref.1) | copy-start | bytes 196
  0.0 18.1 %copy-start = (bf16[512,640]{1,0:T(8,128)(2,1)S(1)}, bf16[512,640]{1,0:T(8,128)(2,1)}, u32[]{:S(2)}) copy-start(bf16[512,640]{1,0:T(8,128)(2,1)} %query_hbm.3) | copy-start | bytes 1966084
  0.0 18.1 %copy-start.1 = (bf16[512,640]{1,0:T(8,128)(2,1)S(1)}, bf16[512,640]{1,0:T(8,128)(2,1)}, u32[]{:S(2)}) copy-start(bf16[512,640]{1,0:T(8,128)(2,1)} %key_hbm.3) | copy-start | bytes 1966084
  0.0 12.6 %copy-start.3 = (f32[640]{0:T(1024)S(1)}, f32[640]{0:T(1024)}, u32[]{:S(2)}) copy-start(f32[640]{0:T(1024)} %param.9) | copy-start | bytes 7684
  0.0 12.7 %copy-start.4 = (f32[640]{0:T(1024)S(1)}, f32[640]{0:T(1024)}, u32[]{:S(2)}) copy-start(f32[640]{0:T(1024)} %param.10) | copy-start | bytes 7684
  2.5 27.5 %collective-permute-start.2 = (bf16[512,640]{1,0:T(8,128)(2,1)S(1)}, bf16[512,640]{1,0:T(8,128)(2,1)S(1)}, u32[]{:S(2)}, u32[]{:S(2)}) collective-permute-start(bf16[512,640]{1,0:T(8,128)(2,1)S(1)} %get-tuple-element.36.ranked_value_ref.refs_1_), channel_id=1, source_target_pairs={{0,1},{1,2},{2,3},{3,4},{4,5},{5,6},{6,7},{7,8},{8,9},{9,10},{10,1... | collective-permute-start | bytes 1966088 | tf_op jit(solution)/shard_map/ppermute | solution.py:21
  6.0 24.1 %collective-permute-start.3 = (bf16[512,640]{1,0:T(8,128)(2,1)S(1)}, bf16[512,640]{1,0:T(8,128)(2,1)S(1)}, u32[]{:S(2)}, u32[]{:S(2)}) collective-permute-start(bf16[512,640]{1,0:T(8,128)(2,1)S(1)} %get-tuple-element.36.ranked_value_ref.refs_1_), channel_id=1, source_target_pairs={{1,0},{2,1},{3,2},{4,3},{5,4},{6,5},{7,6},{8,7},{9,8},{10,9},{11,1... | collective-permute-start | bytes 1966088 | tf_op jit(solution)/shard_map/ppermute | solution.py:21
  8.3 9.8 %all-to-all-start = ((f32[8,2,512]{2,1,0:T(2,128)}), f32[8,2,512]{2,1,0:T(2,128)S(1)}, u32[]{:S(2)}, u32[]{:S(2)}) async-start(f32[8,2,512]{2,1,0:T(2,128)} %get-tuple-element.35), calls=%async_computation | async-start | bytes 65536 | tf_op jit(solution)/shard_map/all_to_all | solution.py:306
  19.8 32.6 %collective-permute-start = (bf16[512,640]{1,0:T(8,128)(2,1)S(1)}, bf16[512,640]{1,0:T(8,128)(2,1)S(1)}, u32[]{:S(2)}, u32[]{:S(2)}) collective-permute-start(bf16[512,640]{1,0:T(8,128)(2,1)S(1)} %get-tuple-element.38.refs_0_), channel_id=1, source_target_pairs={{0,1},{1,2},{2,3},{3,4},{4,5},{5,6},{6,7},{7,8},{8,9},{9,10},{10,1... | collective-permute-start | bytes 1966088 | tf_op jit(solution)/shard_map/ppermute | solution.py:21
  25.4 30.2 %collective-permute-start.1 = (bf16[512,640]{1,0:T(8,128)(2,1)S(1)}, bf16[512,640]{1,0:T(8,128)(2,1)S(1)}, u32[]{:S(2)}, u32[]{:S(2)}) collective-permute-start(bf16[512,640]{1,0:T(8,128)(2,1)S(1)} %get-tuple-element.38.refs_0_), channel_id=1, source_target_pairs={{1,0},{2,1},{3,2},{4,3},{5,4},{6,5},{7,6},{8,7},{9,8},{10,9},{11,1... | collective-permute-start | bytes 1966088 | tf_op jit(solution)/shard_map/ppermute | solution.py:21
  30.0 37.8 %collective-permute-start.6 = (bf16[512,640]{1,0:T(8,128)(2,1)S(1)}, bf16[512,640]{1,0:T(8,128)(2,1)S(1)}, u32[]{:S(2)}, u32[]{:S(2)}) collective-permute-start(bf16[512,640]{1,0:T(8,128)(2,1)S(1)} %get-tuple-element.47), channel_id=1, source_target_pairs={{3,0},{4,1},{5,2},{6,3},{7,4},{8,5},{9,6},{10,7},{11,8},{12,9},{13... | collective-permute-start | bytes 1966088 | tf_op jit(solution)/shard_map/ppermute | solution.py:21
  34.7 36.1 %collective-permute-start.4 = (bf16[512,640]{1,0:T(8,128)(2,1)S(1)}, bf16[512,640]{1,0:T(8,128)(2,1)S(1)}, u32[]{:S(2)}, u32[]{:S(2)}) collective-permute-start(bf16[512,640]{1,0:T(8,128)(2,1)S(1)} %get-tuple-element.47), channel_id=1, source_target_pairs={{0,3},{1,4},{2,5},{3,6},{4,7},{5,8},{6,9},{7,10},{8,11},{9,12},{10... | collective-permute-start | bytes 1966088 | tf_op jit(solution)/shard_map/ppermute | solution.py:21
  55.8 40.8 %collective-permute-start.9 = (bf16[512,640]{1,0:T(8,128)(2,1)S(1)}, bf16[512,640]{1,0:T(8,128)(2,1)S(1)}, u32[]{:S(2)}, u32[]{:S(2)}) collective-permute-start(bf16[512,640]{1,0:T(8,128)(2,1)S(1)} %shard_map.70), channel_id=1, source_target_pairs={{1,0},{2,1},{3,2},{4,3},{5,4},{6,5},{7,6},{8,7},{9,8},{10,9},{11,1... | collective-permute-start | bytes 1966088 | tf_op jit(solution)/shard_map/ppermute | solution.py:21
  60.5 36.2 %collective-permute-start.8 = (bf16[512,640]{1,0:T(8,128)(2,1)S(1)}, bf16[512,640]{1,0:T(8,128)(2,1)S(1)}, u32[]{:S(2)}, u32[]{:S(2)}) collective-permute-start(bf16[512,640]{1,0:T(8,128)(2,1)S(1)} %shard_map.69), channel_id=1, source_target_pairs={{0,1},{1,2},{2,3},{3,4},{4,5},{5,6},{6,7},{7,8},{8,9},{9,10},{10,1... | collective-permute-start | bytes 1966088 | tf_op jit(solution)/shard_map/ppermute | solution.py:21
  64.0 20.1 %collective-permute-start.10 = (bf16[256,640]{1,0:T(8,128)(2,1)S(1)}, bf16[256,640]{1,0:T(8,128)(2,1)S(1)}, u32[]{:S(2)}, u32[]{:S(2)}) collective-permute-start(bf16[256,640]{1,0:T(8,128)(2,1)S(1)} %get-tuple-element.50), channel_id=1, source_target_pairs={{0,4},{1,5},{2,6},{3,7},{4,8},{5,9},{6,10},{7,11},{8,12},{9,13},{1... | collective-permute-start | bytes 983048 | tf_op jit(solution)/shard_map/ppermute | solution.py:21
  67.9 25.0 %collective-permute-start.11 = (bf16[256,640]{1,0:T(8,128)(2,1)S(1)}, bf16[256,640]{1,0:T(8,128)(2,1)S(1)}, u32[]{:S(2)}, u32[]{:S(2)}) collective-permute-start(bf16[256,640]{1,0:T(8,128)(2,1)S(1)} %get-tuple-element.50), channel_id=1, source_target_pairs={{4,0},{5,1},{6,2},{7,3},{8,4},{9,5},{10,6},{11,7},{12,8},{13,9},{1... | collective-permute-start | bytes 983048 | tf_op jit(solution)/shard_map/ppermute | solution.py:21
  70.8 44.6 %collective-permute-start.7 = (bf16[512,640]{1,0:T(8,128)(2,1)S(1)}, bf16[512,640]{1,0:T(8,128)(2,1)S(1)}, u32[]{:S(2)}, u32[]{:S(2)}) collective-permute-start(bf16[512,640]{1,0:T(8,128)(2,1)S(1)} %shard_map.68), channel_id=1, source_target_pairs={{4,0},{5,1},{6,2},{7,3},{8,4},{9,5},{10,6},{11,7},{12,8},{13,9},{1... | collective-permute-start | bytes 1966088 | tf_op jit(solution)/shard_map/ppermute | solution.py:21
  84.2 31.3 %collective-permute-start.5 = (bf16[512,640]{1,0:T(8,128)(2,1)S(1)}, bf16[512,640]{1,0:T(8,128)(2,1)S(1)}, u32[]{:S(2)}, u32[]{:S(2)}) collective-permute-start(bf16[512,640]{1,0:T(8,128)(2,1)S(1)} %shard_map.67), channel_id=1, source_target_pairs={{0,4},{1,5},{2,6},{3,7},{4,8},{5,9},{6,10},{7,11},{8,12},{9,13},{1... | collective-permute-start | bytes 1966088 | tf_op jit(solution)/shard_map/ppermute | solution.py:21
  97.2 13.1 %collective-permute-start.12 = (bf16[256,640]{1,0:T(8,128)(2,1)S(1)}, bf16[256,640]{1,0:T(8,128)(2,1)S(1)}, u32[]{:S(2)}, u32[]{:S(2)}) collective-permute-start(bf16[256,640]{1,0:T(8,128)(2,1)S(1)} %shard_map.73), channel_id=1, source_target_pairs={{0,4},{1,5},{2,6},{3,7},{4,8},{5,9},{6,10},{7,11},{8,12},{9,13},{1... | collective-permute-start | bytes 983048 | tf_op jit(solution)/shard_map/ppermute | solution.py:21
  104.5 11.0 %collective-permute-start.13 = (bf16[256,640]{1,0:T(8,128)(2,1)S(1)}, bf16[256,640]{1,0:T(8,128)(2,1)S(1)}, u32[]{:S(2)}, u32[]{:S(2)}) collective-permute-start(bf16[256,640]{1,0:T(8,128)(2,1)S(1)} %shard_map.74), channel_id=1, source_target_pairs={{4,0},{5,1},{6,2},{7,3},{8,4},{9,5},{10,6},{11,7},{12,8},{13,9},{1... | collective-permute-start | bytes 983048 | tf_op jit(solution)/shard_map/ppermute | solution.py:21
